TPU v7x, 32 devices: a whole 2x2x4 slice. The times are simulated.
32 devices in a mesh: row: 4 (over x, core), col: 8 (over z, y).
Axes of the slice: x: 2, y: 2, z: 4, core: 2. Of those that a mesh axis runs over, the one named last changes fastest.
Arguments:
- design: bfloat16 [512, 14080], P('row', 'col'), may hold values from -0.25 to 0.25
- nuisance_vals: float32 [4, 512], P(None, 'row'), may hold values from -2 to 2
- arc_index: int32 [512], P('row'), may hold values from 0 to 63, never falling along the last dimension, each value on 1 to 16 neighbouring positions
- filter_taps: float32 [128], replicated, may hold values from -0.5 to 0.5
- ordering: int32 [14336], replicated, may hold values from 0 to 14335, each once
- normal_prior: float32 [14336, 14336], P('row', 'col'), may hold values from -0.4 to 25
Outputs:
- normal_post: float32 [14336, 14336], P('row', 'col')
Inputs may be any that keep to these rules, and one draw needn't show every extreme that they name: `arc_index`: arc numbers never fall along the rows; each arc covers 1 to 16 rows. `ordering`: every slot is the image of exactly one design column.
All inputs are finite; a program needn't handle non-finite values.
Results may differ from a plain program's by a relative error of at most 0.0065.
Values may be sent and summed in bfloat16 or wider, within the bound.
No kernel may reach another device: no remote copies, remote signals or barrier semaphores. Data moves between devices by JAX's collectives and lax.ppermute only.
A program may use at most 128 MiB of HBM per device.

v0:
```python
import functools
import math

import jax
import jax.numpy as jnp
from jax import lax
from jax.experimental import pallas as pl
from jax.experimental.pallas import tpu as pltpu
from jax.sharding import PartitionSpec as P


LANES = 128
MIB = 2**20
VM = pl.BlockSpec(memory_space=pltpu.VMEM)
SM = pl.BlockSpec(memory_space=pltpu.SMEM)
HB = pl.BlockSpec(memory_space=pltpu.HBM)
BF, F32, I32 = jnp.bfloat16, jnp.float32, jnp.int32


def capacity(width, groups):
    share = width / groups
    return -(-math.ceil(share + 3.9 * math.sqrt(share * (1 - 1 / groups))) // 16) * 16


def ring_order(count):
    depth = math.gcd(count, 4)
    side = count // depth
    order = [z * side for z in range(depth)]
    for turn, z in enumerate(reversed(range(depth))):
        ys = range(1, side) if turn % 2 == 0 else range(side - 1, 0, -1)
        order += [z * side + y for y in ys]
    return order


def swapped(x, axis, distance):
    return lax.ppermute(x, axis, [(i, i ^ distance) for i in range(lax.axis_size(axis))])


def toeplitz(taps, rows):
    period = 2 * rows + 1
    padded = jnp.concatenate([taps, jnp.zeros((period - taps.shape[0],), F32)])
    return jnp.tile(padded, rows)[: rows * 2 * rows].reshape(rows, 2 * rows)


def kernel_call(body, limit, flops, moved, **kw):
    return pl.pallas_call(
        body,
        compiler_params=pltpu.CompilerParams(vmem_limit_bytes=limit * MIB),
        cost_estimate=pl.CostEstimate(flops=flops, bytes_accessed=moved, transcendentals=0),
        **kw,
    )


def own_slots(order_ref, width):
    chunks = -(-width // LANES)
    total = order_ref.shape[0] * LANES
    begin = lax.axis_index("col") * width
    first, shift = begin // LANES, lax.rem(begin, LANES)
    rows = [order_ref[pl.ds(first + i, 1), :] for i in range(chunks + 1)]
    turn = lax.rem(LANES - shift, LANES)
    near = pltpu.roll(jnp.concatenate(rows[:-1], 0), turn, 1)
    far = pltpu.roll(jnp.concatenate(rows[1:], 0), turn, 1)
    lane = lax.broadcasted_iota(I32, (chunks, LANES), 1)
    index = lax.broadcasted_iota(I32, (chunks, LANES), 0) * LANES + lane
    slots = jnp.where(lane < LANES - shift, near, far)
    return jnp.where(index < width, slots, total)


def select_kernel(axis, share, cap, width, order_ref, raw_ref, *refs):
    outs, full = refs[:-1], refs[-1]
    slots = own_slots(order_ref, width)
    chunks = slots.shape[0]
    full[pl.ds(0, width), :] = raw_ref[...]
    if chunks * LANES > width:
        rest = chunks * LANES - width
        full[pl.ds(width, rest), :] = jnp.zeros((rest, full.shape[1]), BF)
    lane = lambda d: lax.broadcasted_iota(I32, (LANES, LANES), d)
    earlier = jnp.where(lane(0) < lane(1), 1.0, 0.0).astype(BF)
    chunk = lambda d: lax.broadcasted_iota(I32, (chunks, chunks), d)
    above = jnp.where(chunk(1) < chunk(0), 1.0, 0.0).astype(BF)
    buckets = len(outs) if len(outs) > 1 else outs[0].shape[0] // cap

    def bucket(which, store):
        low = which * share
        inside = (slots >= low) & (slots < low + share)
        marks = jnp.where(inside, 1.0, 0.0).astype(BF)
        within = jnp.dot(marks, earlier, preferred_element_type=F32)
        before = jnp.dot(above, marks, preferred_element_type=F32)
        rank = (within + jnp.sum(before, axis=1, keepdims=True)).astype(I32)
        rank = jnp.where(inside, rank, -1)
        row = lax.broadcasted_iota(I32, (cap, LANES), 0)
        hot = jnp.concatenate(
            [
                jnp.where(row == rank[q : q + 1, :], 1.0, 0.0).astype(BF)
                for q in range(chunks)
            ],
            1,
        )
        store(jnp.dot(hot, full[...], preferred_element_type=F32).astype(BF))

    if len(outs) > 1:
        me = lax.axis_index(axis)
        for m, out in enumerate(outs):

            def store(got, out=out):
                out[...] = got

            bucket(m ^ me, store)
    else:

        @pl.loop(0, buckets)
        def _(m):
            def store(got):
                outs[0][pl.ds(pl.multiple_of(m * cap, 16), cap), :] = got

            bucket(m, store)


def select(raw, order, axis, share, cap, buckets, split):
    width, times = raw.shape
    chunks = -(-width // LANES)
    if split:
        shape = [jax.ShapeDtypeStruct((cap, times), BF)] * buckets
    else:
        shape = [jax.ShapeDtypeStruct((buckets * cap, times), BF)]
    return kernel_call(
        functools.partial(select_kernel, axis, share, cap, width),
        12,
        2 * buckets * cap * chunks * LANES * 256,
        2 * (width + buckets * cap) * times,
        out_shape=shape,
        in_specs=[VM, VM],
        out_specs=[VM] * len(shape),
        scratch_shapes=[pltpu.VMEM((chunks * LANES, times), BF)],
    )(order, raw)


def filter_rows(toep_ref, pieces, line, out, begin=0):
    me = lax.axis_index("row")
    times = toep_ref.shape[0]
    taps = jnp.concatenate([toep_ref[:, times:], toep_ref[:, :times]], 0)
    high = taps.astype(BF)
    both = jnp.concatenate([high, (taps - high.astype(F32)).astype(BF)], 1)
    rows, block = out.shape[0], line.shape[0]
    line[:, :times] = jnp.zeros((block, times), BF)

    @pl.loop(0, rows // block)
    def _(i):
        there = pl.ds(pl.multiple_of(i * block, block), block)
        source = pl.ds(pl.multiple_of(begin + i * block, math.gcd(begin, block)), block)
        for m, piece in enumerate(pieces):
            at = pl.ds(pl.multiple_of(((m ^ me) + 1) * times, times), times)
            line[:, at] = piece[source, :]
        for s in range(len(pieces)):
            got = jnp.dot(
                line[:, s * times : (s + 2) * times], both, preferred_element_type=F32
            )
            got = got[:, :times] + got[:, times:]
            out[there, s * times : (s + 1) * times] = got.astype(out.dtype)


def filter_kernel(toep_ref, *refs):
    pieces, out, line = refs[:-2], refs[-2], refs[-1]
    filter_rows(toep_ref, pieces, line, out)


def filtered(pieces, toep):
    rows, times = pieces[0].shape
    count = len(pieces)
    return kernel_call(
        filter_kernel,
        12,
        8 * rows * count * times * times,
        4 * rows * count * times,
        out_shape=jax.ShapeDtypeStruct((rows, count * times), BF),
        in_specs=[VM] * (1 + count),
        out_specs=VM,
        scratch_shapes=[pltpu.VMEM((math.gcd(rows, 256), (count + 1) * times), BF)],
    )(toep, *pieces)


def put_rows(list_ref, begin, rows, panel):
    group = math.gcd(rows.shape[0], 32)

    @pl.loop(0, rows.shape[0] // group)
    def _(g):
        at = pl.multiple_of(g * group, group)
        to = [list_ref[begin + at + q] for q in range(group)]
        values = rows[pl.ds(at, group), :].astype(F32)
        for q in range(group):
            panel[pl.ds(to[q], 1), :] = values[q : q + 1, :]


def bring(copy):
    copy.start()
    copy.wait()


def ring_source(walk_ref, cols, step):
    return walk_ref[lax.axis_index("col") * cols + step]


def first_place_kernel(steps, cols, cap, rounds_ref, walk_ref, list_ref, extra_ref, *refs):
    nuis, old, _, _ = refs[:4]
    shards, (panel, sem) = refs[4:-2], refs[-2:]

    @pl.when(rounds_ref[0] > 1)
    def _():
        bring(pltpu.make_async_copy(old, panel, sem))

    for step, shard in zip(steps, shards):
        put_rows(list_ref, ring_source(walk_ref, cols, step) * cap, shard, panel)
    put_rows(extra_ref, 0, nuis, panel)


def first_place(shards, steps, rounds, walk, listed, extra, nuis, old, after, cols, cap):
    return kernel_call(
        functools.partial(first_place_kernel, steps, cols, cap),
        6,
        0,
        12 * sum(s.size for s in shards),
        out_shape=jax.ShapeDtypeStruct(old.shape, F32),
        in_specs=[SM, SM, SM, SM, VM, HB, SM, SM] + [VM] * len(shards),
        out_specs=VM,
        scratch_shapes=[pltpu.SemaphoreType.DMA],
    )(rounds, walk, listed, extra, nuis, old, *after, *shards)


def place_kernel(steps, cols, cap, walk_ref, list_ref, *refs):
    shards, panel = refs[: len(steps)], refs[-1]
    for step, shard in zip(steps, shards):
        put_rows(list_ref, ring_source(walk_ref, cols, step) * cap, shard, panel)


def place(shards, steps, walk, listed, panel, cols, cap):
    return kernel_call(
        functools.partial(place_kernel, steps, cols, cap),
        6,
        0,
        12 * sum(s.size for s in shards),
        out_shape=jax.ShapeDtypeStruct(panel.shape, F32),
        in_specs=[SM, SM] + [VM] * (len(shards) + 1),
        out_specs=VM,
        input_output_aliases={2 + len(shards): 0},
    )(walk, listed, *shards, panel)


def halves_kernel(half, up, down, first, second):
    first[...] = up[pl.ds(0, half), :]
    second[...] = down[pl.ds(half, second.shape[0]), :]


def halves_of(up, down, half):
    rows, span = up.shape
    return kernel_call(
        functools.partial(halves_kernel, half),
        3,
        0,
        8 * up.size,
        out_shape=[
            jax.ShapeDtypeStruct((half, span), BF),
            jax.ShapeDtypeStruct((rows - half, span), BF),
        ],
        in_specs=[VM, VM],
        out_specs=[VM, VM],
    )(up, down)


def columns_kernel(part, parts, rounds_ref, list_ref, extra_ref, toep_ref, nuis, old, *refs):
    first, last = part == 0, part == parts - 1
    if last:
        pieces, (out, panel, acc, line, sem) = refs[:-5], refs[-5:]
    else:
        pieces, (panel, acc, line, sem) = refs[:-4], refs[-4:]
    rows = acc.shape[0]
    if first:

        @pl.when(rounds_ref[0] > 1)
        def _():
            bring(pltpu.make_async_copy(old, panel, sem))

    filter_rows(toep_ref, pieces, line, acc, part * rows)
    put_rows(list_ref, part * rows, acc, panel)
    if first:
        put_rows(extra_ref, 0, nuis, panel)
    if last:
        wide = out.shape[1]
        for at in range(0, wide, LANES):
            size = min(LANES, wide - at)
            out[:, at : at + size] = panel[at : at + size, :].T.astype(BF)


def columns(part, parts, pieces, rounds, listed, extra, nuis, toep, old):
    rows, times = pieces[0].shape
    rows //= parts
    count = len(pieces)
    high, span = old.shape
    last = part == parts - 1
    outs = [jax.ShapeDtypeStruct((span, high - 8), BF), jax.ShapeDtypeStruct((high, span), F32)]
    held = 4 * rows * span + sum(2 * p.size for p in pieces[4:])
    return kernel_call(
        functools.partial(columns_kernel, part, parts),
        4 + held // MIB,
        8 * rows * span * times,
        12 * rows * span,
        out_shape=outs if last else outs[1],
        in_specs=[SM, SM, SM, VM, VM, HB if part == 0 else VM] + [VM] * count,
        out_specs=[VM, VM] if last else VM,
        input_output_aliases={} if part == 0 else {5: 1 if last else 0},
        scratch_shapes=[
            pltpu.VMEM((rows, span), F32),
            pltpu.VMEM((math.gcd(rows, 256), span + times), BF),
            pltpu.SemaphoreType.DMA,
        ],
    )(rounds, listed, extra, toep, nuis, old, *pieces)


def update_kernel(begins, step, cols, cap, block, parts, walk_ref, list_ref, *refs):
    shards, refs = refs[: len(begins)], refs[len(begins) :]
    weights, priors, (_, out, panel, held, sems) = refs[0], refs[1 : 1 + parts], refs[1 + parts :]
    source = ring_source(walk_ref, cols, step) * cap
    for begin, shard in zip(begins, shards):
        put_rows(list_ref, source + begin, shard, panel)
    slots, wide = held.shape[0], held.shape[2]
    each = priors[0].shape[0] // block

    def drain(i, slot):
        there = out.at[pl.ds(pl.multiple_of(i * block, 8), block), :]
        return pltpu.make_async_copy(held.at[slot], there, sems.at[slot])

    for part, prior in enumerate(priors):

        @pl.loop(part * each, (part + 1) * each)
        def _(i, part=part, prior=prior):
            slot = lax.rem(i, slots)

            @pl.when(i >= slots)
            def _():
                drain(i - slots, slot).wait()

            rows = panel[pl.ds(pl.multiple_of(i * block, 8), block), :].astype(BF)
            at = pl.ds(pl.multiple_of((i - part * each) * block, 8), block)
            for begin in range(0, wide, 2 * LANES):
                tile = pl.ds(begin, min(2 * LANES, wide - begin))
                got = jnp.dot(rows, weights[:, tile], preferred_element_type=F32)
                held[slot, :, tile] = prior[at, tile] + got
            drain(i, slot).start()

    steps = each * parts
    for i in range(max(0, steps - slots), steps):
        drain(i, i % slots).wait()


def update(shards, begins, step, walk, listed, panel, weights, priors, cols, cap):
    part, wide = priors[0].shape
    parts, span = len(priors), weights.shape[0]
    high = part * parts
    block = max(b for b in range(16, 513, 16) if part % b == 0)
    slots = min(2, high // block)
    count = len(shards)
    return kernel_call(
        functools.partial(update_kernel, begins, step, cols, cap, block, parts),
        12,
        2 * high * wide * span,
        8 * high * wide,
        out_shape=[
            jax.ShapeDtypeStruct((high, wide), F32),
            jax.ShapeDtypeStruct(panel.shape, F32),
        ],
        in_specs=[SM, SM] + [VM] * (count + 2 + parts),
        out_specs=[HB, VM],
        input_output_aliases={3 + parts + count: 1},
        scratch_shapes=[
            pltpu.VMEM((slots, block, wide), F32),
            pltpu.SemaphoreType.DMA((slots,)),
        ],
    )(walk, listed, *shards, weights, *priors, panel)[0]


def nuisance_kernel(toep_ref, *refs):
    pieces, out, acc = refs[:-2], refs[-2], refs[-1]
    me = lax.axis_index("row")
    lines, times = pieces[0].shape
    count, params = out.shape[0], lines - 1
    column = lax.broadcasted_iota(I32, (count, times), 0)
    owner = (column // params).astype(F32)
    acc[...] = jnp.zeros_like(acc)
    for m, piece in enumerate(pieces):
        picked = jnp.zeros((count, times), F32)
        for q in range(params):
            picked = jnp.where(lax.rem(column, params) == q, piece[q : q + 1, :], picked)
        raw = jnp.where(piece[params:lines, :] == owner, picked, 0.0)
        got = jnp.dot(
            raw, toep_ref[...], precision=lax.Precision.HIGHEST, preferred_element_type=F32
        )
        at = pl.ds(pl.multiple_of((m ^ me) * times, times), 2 * times)
        acc[:, at] = acc[:, at] + got
    out[...] = acc[:, : out.shape[1]].astype(BF).astype(F32)


def filtered_nuisance(pieces, toep, count):
    groups = len(pieces)
    times = pieces[0].shape[1]
    return kernel_call(
        nuisance_kernel,
        8,
        24 * groups * count * times * times,
        4 * count * groups * times,
        out_shape=jax.ShapeDtypeStruct((count, groups * times), F32),
        in_specs=[VM] * (1 + groups),
        out_specs=VM,
        scratch_shapes=[pltpu.VMEM((count, (groups + 1) * times), F32)],
    )(toep, *pieces)


def keys_kernel(bits, shares, caps, slots_ref, keys, rounds):
    slots = slots_ref[...]
    groups, width = slots.shape
    key = (lax.broadcasted_iota(I32, slots.shape, 1) << bits) | slots
    need = jnp.int32(1)
    for i, (axis, share, cap) in enumerate(zip(("row", "col"), shares, caps)):
        low = lax.axis_index(axis) * share
        inside = (slots >= low) & (slots < low + share)
        keys[i * groups : (i + 1) * groups, :] = jnp.where(inside, key, width << bits)
        most = jnp.zeros((groups, 1), F32)
        for b in range(lax.axis_size(axis)):
            mark = (slots >= b * share) & (slots < (b + 1) * share)
            found = jnp.sum(jnp.where(mark, 1.0, 0.0), axis=1, keepdims=True)
            most = jnp.maximum(most, found)
        need = jnp.maximum(need, (jnp.max(most).astype(I32) + cap - 1) // cap)
    rounds[0] = need


def overflow_round(step, raw, slots, toep, sizes, panels):
    (row_share, cap_row), (col_share, cap_col) = sizes
    times = raw.shape[1]
    rows, cols = lax.axis_size("row"), lax.axis_size("col")
    r, c = lax.axis_index("row"), lax.axis_index("col")
    own = slots[c]

    def buckets(share, cap, groups):
        owner = own // share
        hit = owner == jnp.arange(groups)[:, None]
        rank = jnp.sum(jnp.where(hit, jnp.cumsum(hit.astype(I32), axis=1), 0), axis=0) - 1
        rank = rank - step * cap
        to = jnp.where((rank >= 0) & (rank < cap), owner * cap + rank, -1)
        hot = (jnp.arange(groups * cap)[:, None] == to[None, :]).astype(BF)
        got = jnp.dot(hot, raw, preferred_element_type=F32).astype(BF)
        return got.reshape(groups, cap, times)

    def listing(share, cap, index):
        hit = slots // share == index
        rank = jnp.cumsum(hit.astype(I32), axis=1) - 1
        to = jnp.where(hit, rank - step * cap, -1)
        hot = to[:, None, :] == jnp.arange(cap)[None, :, None]
        code = jnp.where(hot, slots[:, None, :] - index * share + 1, 0)
        found = jnp.sum(code, axis=2)
        return jnp.where(found > 0, found - 1, share)

    def filter_all(x):
        return filtered([lax.dynamic_index_in_dim(x, m ^ r, 0, False) for m in range(rows)], toep)

    def everywhere(x, axis):
        size = lax.axis_size(axis)
        return lax.all_to_all(jnp.broadcast_to(x[None], (size,) + x.shape), axis, 0, 0, tiled=True)

    got = lax.all_to_all(buckets(row_share, cap_row, rows), "row", 0, 0, tiled=True)
    shards = everywhere(filter_all(got), "col")
    held = lax.all_to_all(buckets(col_share, cap_col, cols), "col", 0, 0, tiled=True)
    held = filter_all(everywhere(held.reshape(cols * cap_col, times), "row"))
    row_list = listing(row_share, cap_row, r).reshape(-1)
    col_list = listing(col_share, cap_col, c).reshape(-1)
    span = held.shape[1]
    return (
        panels[0].at[row_list].set(shards.reshape(-1, span).astype(F32)),
        panels[1].at[col_list].set(held.astype(F32)),
    )


def per_device(design, nuisance_vals, arc_index, filter_taps, ordering, normal_prior):
    times, width = design.shape
    rows, cols = lax.axis_size("row"), lax.axis_size("col")
    total = ordering.shape[0]
    row_share, col_share = total // rows, total // cols
    span = rows * times
    extras = total - width * cols
    cap_row, cap_col = capacity(width, rows), capacity(width, cols)

    raw = design.T
    order2d = ordering.reshape(total // LANES, LANES)
    to_rows = select(raw, order2d, "row", row_share, cap_row, rows, True)
    pieces = [to_rows[0]] + [swapped(to_rows[m], "row", m) for m in range(1, rows)]
    params = jnp.concatenate([nuisance_vals, arc_index.astype(F32)[None]], 0)
    params, _ = lax.optimization_barrier((params, to_rows[-1]))
    params = [params] + [swapped(params, "row", m) for m in range(1, rows)]
    late, _ = lax.optimization_barrier((raw, to_rows[-1]))
    (to_cols,) = select(late, order2d, "col", col_share, cap_col, cols, False)
    toep = toeplitz(filter_taps, times)
    *pieces, _ = lax.optimization_barrier((*pieces, to_cols))
    shard = filtered(pieces, toep)
    to_cols, _ = lax.optimization_barrier((to_cols, shard))
    mine = lax.all_to_all(to_cols, "col", 0, 0, tiled=True)

    ordering, _ = lax.optimization_barrier((ordering, shard))
    slots = ordering[: width * cols].reshape(cols, width)
    bits = (total - 1).bit_length()
    keys, rounds = kernel_call(
        functools.partial(
            keys_kernel, bits, (row_share, col_share), (cap_row, cap_col)
        ),
        4,
        0,
        12 * width * cols,
        out_shape=[
            jax.ShapeDtypeStruct((2 * cols, width), I32),
            jax.ShapeDtypeStruct((1,), I32),
        ],
        in_specs=[VM],
        out_specs=[VM, SM],
    )(slots)
    order = ring_order(cols)
    ahead = [(order[i], order[(i + 1) % cols]) for i in range(cols)]
    back = [(b, a) for a, b in ahead]
    walk = jnp.array(
        [order[(order.index(i) + j) % cols] for i in range(cols) for j in range(cols)], I32
    )

    up = lax.ppermute(shard, "col", ahead)
    down = lax.ppermute(shard, "col", back)
    keys = lax.sort(keys, dimension=1)
    low_row = (lax.axis_index("row") * row_share).astype(I32)
    low_col = (lax.axis_index("col") * col_share).astype(I32)

    def listing(part, low, share, cap):
        part = part[:, :cap]
        found = (part & ((1 << bits) - 1)) - low
        return jnp.where(part < (width << bits), found, share).reshape(-1)

    row_list = listing(keys[:cols], low_row, row_share, cap_row)
    col_list = listing(keys[cols:], low_col, col_share, cap_col)

    def extra_list(low, share):
        at = ordering[width * cols :] - low
        return jnp.where((at >= 0) & (at < share), at, share)

    nuis = filtered_nuisance(params, toep, extras)

    shapes = [(row_share + 8, span), (col_share + 8, span)]
    empty = kernel_call(
        lambda *refs: None,
        1,
        0,
        0,
        out_shape=[jax.ShapeDtypeStruct(s, F32) for s in shapes],
        out_specs=[HB, HB],
    )()
    sizes = ((row_share, cap_row), (col_share, cap_col))

    def more(carry):
        return carry[0] < rounds[0]

    def again(carry):
        step, *panels = carry
        panels = overflow_round(step, raw, slots, toep, sizes, panels)
        return (step + 1, *panels)

    _, old_rows, old_cols = lax.while_loop(more, again, (jnp.int32(1), *empty))

    parts = {0: mine}
    distance = rows // 2
    while distance:
        for m in list(parts):
            parts[m ^ distance] = swapped(parts[m], "row", distance)
        distance //= 2

    steps, half = cols // 2, cap_row // 2
    half -= half % 16
    row_extra = extra_list(low_row, row_share)
    col_extra = extra_list(low_col, col_share)
    halves = [parts[m] for m in range(rows)]

    def column_part(part, panel):
        return columns(part, 2, halves, rounds, col_list, col_extra, nuis, toep, panel)

    panel = None
    batch, at = [], []
    for i in range(1, steps):
        if i > 1:
            up = lax.ppermute(up, "col", ahead)
            down = lax.ppermute(down, "col", back)
            if panel is None:
                panel = first_place(
                    [shard],
                    [0],
                    rounds,
                    walk,
                    row_list,
                    row_extra,
                    nuis,
                    old_rows,
                    (col_list, col_extra),
                    cols,
                    cap_row,
                )
            panel = place(batch, at, walk, row_list, panel, cols, cap_row)
            batch, at = [], []
        batch += [up, down]
        at += [(cols - i) % cols, i]
    col_panel = column_part(0, old_cols)
    up, down = halves_of(up, down, half)
    up = lax.ppermute(up, "col", ahead)
    down = lax.ppermute(down, "col", back)
    panel = place(batch, at, walk, row_list, panel, cols, cap_row)
    weights, _ = column_part(1, col_panel)
    return update(
        [up, down],
        (0, half),
        steps,
        walk,
        row_list,
        panel,
        weights,
        [normal_prior],
        cols,
        cap_row,
    )


def solution(mesh):
    return jax.shard_map(
        per_device,
        mesh=mesh,
        in_specs=(P("row", "col"), P(None, "row"), P("row"), P(), P(), P("row", "col")),
        out_specs=P("row", "col"),
        check_vma=False,
    )
```

profile of v0, /device:TPU:0, one launch (start us, length us, event | category | flops | bytes accessed | tf_op | source)
XLA Modules:
  0.0 115.4 jit_solution(12180669832377584597)
XLA Ops:
  0.0 4.7 %shard_map.73 = (bf16[512,128]{1,0:T(8,128)(2,1)S(1)}, bf16[512,128]{1,0:T(8,128)(2,1)S(1)}, bf16[512,128]{1,0:T(8,128)(2,1)S(1)}, bf16[512,128]{1,0:T(8,128)(2,1)S(1)}) custom-call(s32[112,128]{1,0:T(8,128)} %bitcast.143, bf16[1760,128]{1,0:T(8,128)(2,1)} %bitcast.153), custom_call_target="tpu_custom_call" | custom-call | flops 1879048192 | bytes 974848 | tf_op jit(solution)/shard_map/pallas_call | solution.py:126
  5.3 2.6 %collective-permute-start.1 = (bf16[512,128]{1,0:T(8,128)(2,1)S(1)}, bf16[512,128]{1,0:T(8,128)(2,1)S(1)}, u32[]{:S(2)}, u32[]{:S(2)}) collective-permute-start(bf16[512,128]{1,0:T(8,128)(2,1)S(1)} %get-tuple-element.178), channel_id=1, source_target_pairs={{0,16},{8,24},{16,0},{24,8},{1,17},{9,25},{17,1},{25,9},{2,18},{10... | collective-permute-start | bytes 393224 | tf_op jit(solution)/shard_map/ppermute | solution.py:36
  9.0 5.8 %shard_map.74 = bf16[2304,128]{1,0:T(8,128)(2,1)} custom-call(s32[112,128]{1,0:T(8,128)S(1)} %bitcast.145, bf16[1760,128]{1,0:T(8,128)(2,1)S(1)} %bitcast.155), custom_call_target="tpu_custom_call" | custom-call | flops 2113929216 | bytes 1040384 | tf_op jit(solution)/shard_map/pallas_call | solution.py:126
  15.4 1.9 %collective-permute-start.6 = (bf16[512,512]{1,0:T(8,128)(2,1)S(1)}, bf16[512,512]{1,0:T(8,128)(2,1)S(1)}, u32[]{:S(2)}, u32[]{:S(2)}) collective-permute-start(bf16[512,512]{1,0:T(8,128)(2,1)S(1)} %shard_map.75.refs_4_), channel_id=1, source_target_pairs={{2,0},{4,2},{6,4},{7,6},{5,7},{3,5},{1,3},{0,1},{10,8},{12,10},{14... | collective-permute-start | bytes 1572872 | tf_op jit(solution)/shard_map/ppermute | solution.py:529
  17.5 6.1 %all-to-all-start.4 = ((bf16[8,288,128]{2,1,0:T(8,128)(2,1)}), bf16[8,288,128]{2,1,0:T(8,128)(2,1)S(1)}, u32[]{:S(2)}, u32[]{:S(2)}) async-start(bf16[8,288,128]{2,1,0:T(8,128)(2,1)} %bitcast.20), calls=%async_computation.4 | async-start | bytes 1179648 | tf_op jit(solution)/shard_map/all_to_all | solution.py:502
  23.6 7.5 %collective-permute-done.6.refs_1_ = bf16[512,512]{1,0:T(8,128)(2,1)S(1)} collective-permute-done((bf16[512,512]{1,0:T(8,128)(2,1)S(1)}, bf16[512,512]{1,0:T(8,128)(2,1)S(1)}, u32[]{:S(2)}, u32[]{:S(2)}) %collective-permute-start.6) | collective-permute-done | bytes 524320 | tf_op jit(solution)/shard_map/ppermute | solution.py:529
  31.1 2.6 %collective-permute-start.7 = (bf16[512,512]{1,0:T(8,128)(2,1)S(1)}, bf16[512,512]{1,0:T(8,128)(2,1)S(1)}, u32[]{:S(2)}, u32[]{:S(2)}) collective-permute-start(bf16[512,512]{1,0:T(8,128)(2,1)S(1)} %collective-permute-done.6.refs_1_), channel_id=1, source_target_pairs={{2,0},{4,2},{6,4},{7,6},{5,7},{3,5},{1,3},{0,1},{10,8},{12,10},{14... | collective-permute-start | bytes 1572872 | tf_op jit(solution)/shard_map/ppermute | solution.py:590
  33.9 1.5 %collective-permute-start.12 = (f32[5,128]{1,0:T(8,128)S(1)}, f32[5,128]{1,0:T(8,128)S(1)}, u32[]{:S(2)}, u32[]{:S(2)}) collective-permute-start(f32[5,128]{1,0:T(8,128)S(1)} %pad_maximum_fusion.refs_0_), channel_id=1, source_target_pairs={{0,16},{8,24},{16,0},{24,8},{1,17},{9,25},{17,1},{25,9},{2,18},{10... | collective-permute-start | bytes 7688 | tf_op jit(solution)/shard_map/ppermute | solution.py:36
  35.7 1.2 %collective-permute-done.13.refs_3_ = f32[5,128]{1,0:T(8,128)S(1)} collective-permute-done((f32[5,128]{1,0:T(8,128)S(1)}, f32[5,128]{1,0:T(8,128)S(1)}, u32[]{:S(2)}, u32[]{:S(2)}) %collective-permute-start.13) | collective-permute-done | bytes 2592 | tf_op jit(solution)/shard_map/ppermute | solution.py:36
  37.5 1.2 %shard_map.78.nuis.refs_0_ = f32[256,512]{1,0:T(8,128)S(1)} custom-call(f32[128,256]{1,0:T(8,128)S(1)} %reshape.343.toep_ref, f32[5,128]{1,0:T(8,128)S(1)} %pad_maximum_fusion.refs_0_, f32[5,128]{1,0:T(8,128)S(1)} %collective-permute-done.11.refs_1_, f32[5,128]{1,0:T(8,128)S(1)} %collective-permute-done.12.refs_2_, f32[5,128]{1,0:T(8,128)S(1)} %collective-permute-done.13.refs_3_), custom_call_target="tpu_custom_call" | custom-call | flops 402653184 | bytes 524288 | tf_op jit(solution)/shard_map/pallas_call | solution.py:404
  40.2 7.3 %sort.14 = (s32[16,1760]{1,0:T(8,128)}, s32[16,1760]{1,0:T(8,128)}) sort(s32[16,1760]{1,0:T(8,128)S(1)} %get-tuple-element.186, s32[16,1760]{1,0:T(8,128)} %iota.51), dimensions={1}, to_apply=%region_0.0 | sort | flops 422400 | bytes 450560 | tf_op jit(solution)/shard_map/sort | solution.py:530
  47.6 1.4 %collective-permute-start.15 = (bf16[2304,128]{1,0:T(8,128)(2,1)S(1)}, bf16[2304,128]{1,0:T(8,128)(2,1)}, u32[]{:S(2)}, u32[]{:S(2)}) collective-permute-start(bf16[2304,128]{1,0:T(8,128)(2,1)S(1)} %bitcast.127), channel_id=1, source_target_pairs={{0,16},{8,24},{16,0},{24,8},{1,17},{9,25},{17,1},{25,9},{2,18},{10... | collective-permute-start | bytes 1769480 | tf_op jit(solution)/shard_map/ppermute | solution.py:36
  49.0 1.5 %collective-permute-done.7.refs_1_ = bf16[512,512]{1,0:T(8,128)(2,1)S(1)} collective-permute-done((bf16[512,512]{1,0:T(8,128)(2,1)S(1)}, bf16[512,512]{1,0:T(8,128)(2,1)S(1)}, u32[]{:S(2)}, u32[]{:S(2)}) %collective-permute-start.7) | collective-permute-done | bytes 524320 | tf_op jit(solution)/shard_map/ppermute | solution.py:590
  51.3 4.1 %collective-permute-start.5 = (bf16[512,512]{1,0:T(8,128)(2,1)}, bf16[512,512]{1,0:T(8,128)(2,1)S(1)}, u32[]{:S(2)}, u32[]{:S(2)}) collective-permute-start(bf16[512,512]{1,0:T(8,128)(2,1)} %collective-permute-done.4.refs_0_), channel_id=1, source_target_pairs={{0,2},{2,4},{4,6},{6,7},{7,5},{5,3},{3,1},{1,0},{8,10},{10,12},{12... | collective-permute-start | bytes 1572872 | tf_op jit(solution)/shard_map/ppermute | solution.py:589
  58.3 8.8 %collective-permute-done.8.down.refs_1_ = bf16[512,512]{1,0:T(8,128)(2,1)S(1)} collective-permute-done((bf16[512,512]{1,0:T(8,128)(2,1)S(1)}, bf16[512,512]{1,0:T(8,128)(2,1)S(1)}, u32[]{:S(2)}, u32[]{:S(2)}) %collective-permute-start.8) | collective-permute-done | bytes 524320 | tf_op jit(solution)/shard_map/ppermute | solution.py:590
  68.5 1.4 %collective-permute-start.9 = (bf16[256,512]{1,0:T(8,128)(2,1)}, bf16[256,512]{1,0:T(8,128)(2,1)}, u32[]{:S(2)}, u32[]{:S(2)}) collective-permute-start(bf16[256,512]{1,0:T(8,128)(2,1)} %get-tuple-element.188), channel_id=1, source_target_pairs={{0,2},{2,4},{4,6},{6,7},{7,5},{5,3},{3,1},{1,0},{8,10},{10,12},{12... | collective-permute-start | bytes 786440 | tf_op jit(solution)/shard_map/ppermute | solution.py:611
  70.0 1.2 %collective-permute-start.10 = (bf16[256,512]{1,0:T(8,128)(2,1)}, bf16[256,512]{1,0:T(8,128)(2,1)}, u32[]{:S(2)}, u32[]{:S(2)}) collective-permute-start(bf16[256,512]{1,0:T(8,128)(2,1)} %get-tuple-element.189), channel_id=1, source_target_pairs={{2,0},{4,2},{6,4},{7,6},{5,7},{3,5},{1,3},{0,1},{10,8},{12,10},{14... | collective-permute-start | bytes 786440 | tf_op jit(solution)/shard_map/ppermute | solution.py:612
  73.0 3.2 %shard_map.82.refs_2_ = f32[3592,512]{1,0:T(8,128)S(1)} custom-call(s32[1]{0:T(128)} %get-tuple-element.334.rounds_ref, s32[64]{0:T(128)S(1)} %copy-done.12, s32[4096]{0:T(1024)S(1)} %bitcast.131, s32[256]{0:T(256)S(1)} %get-tuple-element.237.extra_ref, f32[256,512]{1,0:T(8,128)S(1)} %shard_map.78.nuis.refs_0_, f32[3592,512]{1,0:T(8,128)} %get-tuple-element.197.refs_1_, ...), custom_call_target="tpu_custom_call" | custom-call | bytes 3145728 | tf_op jit(solution)/shard_map/pallas_call | solution.py:217
  76.3 2.9 %shard_map.83.refs_2_ = f32[3592,512]{1,0:T(8,128)S(1)} custom-call(s32[64]{0:T(128)S(1)} %copy-done.12, s32[4096]{0:T(1024)S(1)} %bitcast.132, bf16[512,512]{1,0:T(8,128)(2,1)S(1)} %copy-done.9, bf16[512,512]{1,0:T(8,128)(2,1)S(1)} %copy-done.7, f32[3592,512]{1,0:T(8,128)S(1)} %shard_map.82.refs_2_), custom_call_target="tpu_custom_call", output_to_operand_aliasing={{}: (4, {})} | custom-call | bytes 6291456 | tf_op jit(solution)/shard_map/pallas_call | solution.py:236
  79.3 3.3 %shard_map.84.refs_2_ = f32[3592,512]{1,0:T(8,128)S(1)} custom-call(s32[64]{0:T(128)S(1)} %copy-done.12, s32[4096]{0:T(1024)S(1)} %bitcast.133, bf16[512,512]{1,0:T(8,128)(2,1)} %collective-permute-done.4.refs_0_, bf16[512,512]{1,0:T(8,128)(2,1)S(1)} %copy-done.11, f32[3592,512]{1,0:T(8,128)S(1)} %shard_map.83.refs_2_), custom_call_target="tpu_custom_call", output_to_operand_aliasing={{}: (4, {})} | custom-call | bytes 6291456 | tf_op jit(solution)/shard_map/pallas_call | solution.py:236
  82.6 2.9 %shard_map.85.refs_4_ = f32[3592,512]{1,0:T(8,128)S(1)} custom-call(s32[64]{0:T(128)S(1)} %copy-done.12, s32[4096]{0:T(1024)S(1)} %bitcast.134, bf16[512,512]{1,0:T(8,128)(2,1)S(1)} %copy-done.3, bf16[512,512]{1,0:T(8,128)(2,1)S(1)} %copy-done.1, f32[3592,512]{1,0:T(8,128)S(1)} %shard_map.84.refs_2_), custom_call_target="tpu_custom_call", output_to_operand_aliasing={{}: (4, {})} | custom-call | bytes 6291456 | tf_op jit(solution)/shard_map/pallas_call | solution.py:236
  85.6 8.6 %shard_map.80.old = f32[1800,512]{1,0:T(8,128)S(1)} custom-call(s32[1]{0:T(128)} %get-tuple-element.334.rounds_ref, s32[2304]{0:T(1024)S(1)} %reshape.347.list_ref.refs_2_, s32[256]{0:T(256)S(1)} %get-tuple-element.238.extra_ref.refs_3_, f32[128,256]{1,0:T(8,128)S(1)} %get-tuple-element.422, f32[256,512]{1,0:T(8,128)S(1)} %shard_map.78.nuis.refs_0_, ...), custom_call_target="tpu_custom_call" | custom-call | flops 603979776 | bytes 7077888 | tf_op jit(solution)/shard_map/pallas_call | solution.py:301
  94.2 7.0 %shard_map.81 = (bf16[512,1792]{1,0:T(8,128)(2,1)S(1)}, f32[1800,512]{1,0:T(8,128)S(1)}) custom-call(s32[1]{0:T(128)} %get-tuple-element.334.rounds_ref, s32[2304]{0:T(1024)S(1)} %reshape.347.list_ref.refs_2_, s32[256]{0:T(256)S(1)} %get-tuple-element.238.extra_ref.refs_3_, f32[128,256]{1,0:T(8,128)S(1)} %get-tuple-element.422, ...), custom_call_target="tpu_custom_call", output_to_operand_aliasing={{1}: (5, {})} | custom-call | flops 603979776 | bytes 7077888 | tf_op jit(solution)/shard_map/pallas_call | solution.py:301
  101.3 14.0 %shard_map.86 = (f32[3584,1792]{1,0:T(8,128)}, f32[3592,512]{1,0:T(8,128)S(1)}) custom-call(s32[64]{0:T(128)S(1)} %copy-done.12, s32[4096]{0:T(1024)S(1)} %bitcast.135, bf16[256,512]{1,0:T(8,128)(2,1)} %collective-permute-done.9.refs_0_, bf16[256,512]{1,0:T(8,128)(2,1)} %collective-permute-done.10.refs_1_, ...), custom_call_target="tpu_custom_call", output_to_operand_aliasing={{1}: (6, {})} | custom-call | flops 6576668672 | bytes 51380224 | tf_op jit(solution)/shard_map/pallas_call | solution.py:361
  (94 shorter events, 12.2 us)
Async XLA Ops:
  4.7 29.1 %copy-start.23 = (s32[128]{0:T(128)S(1)}, s32[128]{0:T(128)}, u32[]{:S(2)}) copy-start(s32[128]{0:T(128)} %param.11) | copy-start | bytes 1540
  4.7 29.1 %copy-start.21 = (f32[4,128]{1,0:T(4,128)S(1)}, f32[4,128]{1,0:T(4,128)}, u32[]{:S(2)}) copy-start(f32[4,128]{1,0:T(4,128)} %param.10) | copy-start | bytes 6148
  4.7 10.0 %collective-permute-start = (bf16[512,128]{1,0:T(8,128)(2,1)S(1)}, bf16[512,128]{1,0:T(8,128)(2,1)S(1)}, u32[]{:S(2)}, u32[]{:S(2)}) collective-permute-start(bf16[512,128]{1,0:T(8,128)(2,1)S(1)} %get-tuple-element.177), channel_id=1, source_target_pairs={{0,8},{8,0},{16,24},{24,16},{1,9},{9,1},{17,25},{25,17},{2,10},{10... | collective-permute-start | bytes 393224 | tf_op jit(solution)/shard_map/ppermute | solution.py:36
  5.3 9.5 %collective-permute-start.1 = (bf16[512,128]{1,0:T(8,128)(2,1)S(1)}, bf16[512,128]{1,0:T(8,128)(2,1)S(1)}, u32[]{:S(2)}, u32[]{:S(2)}) collective-permute-start(bf16[512,128]{1,0:T(8,128)(2,1)S(1)} %get-tuple-element.178), channel_id=1, source_target_pairs={{0,16},{8,24},{16,0},{24,8},{1,17},{9,25},{17,1},{25,9},{2,18},{10... | collective-permute-start | bytes 393224 | tf_op jit(solution)/shard_map/ppermute | solution.py:36
  7.8 6.9 %collective-permute-start.2 = (bf16[512,128]{1,0:T(8,128)(2,1)S(1)}, bf16[512,128]{1,0:T(8,128)(2,1)S(1)}, u32[]{:S(2)}, u32[]{:S(2)}) collective-permute-start(bf16[512,128]{1,0:T(8,128)(2,1)S(1)} %get-tuple-element.179), channel_id=1, source_target_pairs={{0,24},{8,16},{16,8},{24,0},{1,25},{9,17},{17,9},{25,1},{2,26},{10... | collective-permute-start | bytes 393224 | tf_op jit(solution)/shard_map/ppermute | solution.py:36
  15.4 33.6 %copy-start.4 = (bf16[512,512]{1,0:T(8,128)(2,1)}, bf16[512,512]{1,0:T(8,128)(2,1)S(1)}, u32[]{:S(2)}) copy-start(bf16[512,512]{1,0:T(8,128)(2,1)S(1)} %shard_map.75.refs_4_) | copy-start | bytes 1572868
  15.4 15.7 %collective-permute-start.6 = (bf16[512,512]{1,0:T(8,128)(2,1)S(1)}, bf16[512,512]{1,0:T(8,128)(2,1)S(1)}, u32[]{:S(2)}, u32[]{:S(2)}) collective-permute-start(bf16[512,512]{1,0:T(8,128)(2,1)S(1)} %shard_map.75.refs_4_), channel_id=1, source_target_pairs={{2,0},{4,2},{6,4},{7,6},{5,7},{3,5},{1,3},{0,1},{10,8},{12,10},{14... | collective-permute-start | bytes 1572872 | tf_op jit(solution)/shard_map/ppermute | solution.py:529
  17.3 16.4 %collective-permute-start.3 = (bf16[512,512]{1,0:T(8,128)(2,1)S(1)}, bf16[512,512]{1,0:T(8,128)(2,1)S(1)}, u32[]{:S(2)}, u32[]{:S(2)}) collective-permute-start(bf16[512,512]{1,0:T(8,128)(2,1)S(1)} %shard_map.75.refs_4_), channel_id=1, source_target_pairs={{0,2},{2,4},{4,6},{6,7},{7,5},{5,3},{3,1},{1,0},{8,10},{10,12},{12... | collective-permute-start | bytes 1572872 | tf_op jit(solution)/shard_map/ppermute | solution.py:528
  17.5 30.1 %all-to-all-start.4 = ((bf16[8,288,128]{2,1,0:T(8,128)(2,1)}), bf16[8,288,128]{2,1,0:T(8,128)(2,1)S(1)}, u32[]{:S(2)}, u32[]{:S(2)}) async-start(bf16[8,288,128]{2,1,0:T(8,128)(2,1)} %bitcast.20), calls=%async_computation.4 | async-start | bytes 1179648 | tf_op jit(solution)/shard_map/all_to_all | solution.py:502
  31.1 19.4 %collective-permute-start.7 = (bf16[512,512]{1,0:T(8,128)(2,1)S(1)}, bf16[512,512]{1,0:T(8,128)(2,1)S(1)}, u32[]{:S(2)}, u32[]{:S(2)}) collective-permute-start(bf16[512,512]{1,0:T(8,128)(2,1)S(1)} %collective-permute-done.6.refs_1_), channel_id=1, source_target_pairs={{2,0},{4,2},{6,4},{7,6},{5,7},{3,5},{1,3},{0,1},{10,8},{12,10},{14... | collective-permute-start | bytes 1572872 | tf_op jit(solution)/shard_map/ppermute | solution.py:590
  33.7 37.4 %copy-start.8 = (bf16[512,512]{1,0:T(8,128)(2,1)}, bf16[512,512]{1,0:T(8,128)(2,1)S(1)}, u32[]{:S(2)}) copy-start(bf16[512,512]{1,0:T(8,128)(2,1)S(1)} %collective-permute-done.3.refs_0_) | copy-start | bytes 1572868
  33.7 17.6 %collective-permute-start.4 = (bf16[512,512]{1,0:T(8,128)(2,1)S(1)}, bf16[512,512]{1,0:T(8,128)(2,1)}, u32[]{:S(2)}, u32[]{:S(2)}) collective-permute-start(bf16[512,512]{1,0:T(8,128)(2,1)S(1)} %collective-permute-done.3.refs_0_), channel_id=1, source_target_pairs={{0,2},{2,4},{4,6},{6,7},{7,5},{5,3},{3,1},{1,0},{8,10},{10,12},{12... | collective-permute-start | bytes 1572872 | tf_op jit(solution)/shard_map/ppermute | solution.py:589
  33.8 3.1 %collective-permute-start.13 = (f32[5,128]{1,0:T(8,128)S(1)}, f32[5,128]{1,0:T(8,128)S(1)}, u32[]{:S(2)}, u32[]{:S(2)}) collective-permute-start(f32[5,128]{1,0:T(8,128)S(1)} %pad_maximum_fusion.refs_0_), channel_id=1, source_target_pairs={{0,24},{8,16},{16,8},{24,0},{1,25},{9,17},{17,9},{25,1},{2,26},{10... | collective-permute-start | bytes 7688 | tf_op jit(solution)/shard_map/ppermute | solution.py:36
  33.9 3.7 %collective-permute-start.12 = (f32[5,128]{1,0:T(8,128)S(1)}, f32[5,128]{1,0:T(8,128)S(1)}, u32[]{:S(2)}, u32[]{:S(2)}) collective-permute-start(f32[5,128]{1,0:T(8,128)S(1)} %pad_maximum_fusion.refs_0_), channel_id=1, source_target_pairs={{0,16},{8,24},{16,0},{24,8},{1,17},{9,25},{17,1},{25,9},{2,18},{10... | collective-permute-start | bytes 7688 | tf_op jit(solution)/shard_map/ppermute | solution.py:36
  35.4 2.2 %collective-permute-start.11 = (f32[5,128]{1,0:T(8,128)S(1)}, f32[5,128]{1,0:T(8,128)S(1)}, u32[]{:S(2)}, u32[]{:S(2)}) collective-permute-start(f32[5,128]{1,0:T(8,128)S(1)} %pad_maximum_fusion.refs_0_), channel_id=1, source_target_pairs={{0,8},{8,0},{16,24},{24,16},{1,9},{9,1},{17,25},{25,17},{2,10},{10... | collective-permute-start | bytes 7688 | tf_op jit(solution)/shard_map/ppermute | solution.py:36
  47.6 23.6 %collective-permute-start.15 = (bf16[2304,128]{1,0:T(8,128)(2,1)S(1)}, bf16[2304,128]{1,0:T(8,128)(2,1)}, u32[]{:S(2)}, u32[]{:S(2)}) collective-permute-start(bf16[2304,128]{1,0:T(8,128)(2,1)S(1)} %bitcast.127), channel_id=1, source_target_pairs={{0,16},{8,24},{16,0},{24,8},{1,17},{9,25},{17,1},{25,9},{2,18},{10... | collective-permute-start | bytes 1769480 | tf_op jit(solution)/shard_map/ppermute | solution.py:36
  50.5 16.6 %collective-permute-start.8 = (bf16[512,512]{1,0:T(8,128)(2,1)S(1)}, bf16[512,512]{1,0:T(8,128)(2,1)S(1)}, u32[]{:S(2)}, u32[]{:S(2)}) collective-permute-start(bf16[512,512]{1,0:T(8,128)(2,1)S(1)} %collective-permute-done.7.refs_1_), channel_id=1, source_target_pairs={{2,0},{4,2},{6,4},{7,6},{5,7},{3,5},{1,3},{0,1},{10,8},{12,10},{14... | collective-permute-start | bytes 1572872 | tf_op jit(solution)/shard_map/ppermute | solution.py:590
  51.3 16.4 %collective-permute-start.5 = (bf16[512,512]{1,0:T(8,128)(2,1)}, bf16[512,512]{1,0:T(8,128)(2,1)S(1)}, u32[]{:S(2)}, u32[]{:S(2)}) collective-permute-start(bf16[512,512]{1,0:T(8,128)(2,1)} %collective-permute-done.4.refs_0_), channel_id=1, source_target_pairs={{0,2},{2,4},{4,6},{6,7},{7,5},{5,3},{3,1},{1,0},{8,10},{10,12},{12... | collective-permute-start | bytes 1572872 | tf_op jit(solution)/shard_map/ppermute | solution.py:589
  58.3 27.3 %collective-permute-start.14 = (bf16[2304,128]{1,0:T(8,128)(2,1)S(1)}, bf16[2304,128]{1,0:T(8,128)(2,1)}, u32[]{:S(2)}, u32[]{:S(2)}) collective-permute-start(bf16[2304,128]{1,0:T(8,128)(2,1)S(1)} %bitcast.128), channel_id=1, source_target_pairs={{0,8},{8,0},{16,24},{24,16},{1,9},{9,1},{17,25},{25,17},{2,10},{10... | collective-permute-start | bytes 1769480 | tf_op jit(solution)/shard_map/ppermute | solution.py:36
  68.5 32.6 %collective-permute-start.9 = (bf16[256,512]{1,0:T(8,128)(2,1)}, bf16[256,512]{1,0:T(8,128)(2,1)}, u32[]{:S(2)}, u32[]{:S(2)}) collective-permute-start(bf16[256,512]{1,0:T(8,128)(2,1)} %get-tuple-element.188), channel_id=1, source_target_pairs={{0,2},{2,4},{4,6},{6,7},{7,5},{5,3},{3,1},{1,0},{8,10},{10,12},{12... | collective-permute-start | bytes 786440 | tf_op jit(solution)/shard_map/ppermute | solution.py:611
  70.0 31.2 %collective-permute-start.10 = (bf16[256,512]{1,0:T(8,128)(2,1)}, bf16[256,512]{1,0:T(8,128)(2,1)}, u32[]{:S(2)}, u32[]{:S(2)}) collective-permute-start(bf16[256,512]{1,0:T(8,128)(2,1)} %get-tuple-element.189), channel_id=1, source_target_pairs={{2,0},{4,2},{6,4},{7,6},{5,7},{3,5},{1,3},{0,1},{10,8},{12,10},{14... | collective-permute-start | bytes 786440 | tf_op jit(solution)/shard_map/ppermute | solution.py:612
  71.1 14.4 %collective-permute-start.16 = (bf16[2304,128]{1,0:T(8,128)(2,1)}, bf16[2304,128]{1,0:T(8,128)(2,1)}, u32[]{:S(2)}, u32[]{:S(2)}) collective-permute-start(bf16[2304,128]{1,0:T(8,128)(2,1)} %collective-permute-done.15.refs_2_), channel_id=1, source_target_pairs={{0,8},{8,0},{16,24},{24,16},{1,9},{9,1},{17,25},{25,17},{2,10},{10... | collective-permute-start | bytes 1769480 | tf_op jit(solution)/shard_map/ppermute | solution.py:36
  79.3 21.9 %slice-start = ((s8[25690112]{0:T(1024)(128)(4,1)}), s8[4194304]{0:T(1024)(128)(4,1)S(1)}, s32[]{:S(2)}) async-start(s8[25690112]{0:T(1024)(128)(4,1)} %bitcast.125), calls=%async_computation.5 | async-start | bytes 8388608
  79.3 21.9 %slice-start.1 = ((s8[25690112]{0:T(1024)(128)(4,1)}), s8[4194304]{0:T(1024)(128)(4,1)S(1)}, s32[]{:S(2)}) async-start(s8[25690112]{0:T(1024)(128)(4,1)} %bitcast.125), calls=%async_computation.6 | async-start | bytes 8388608
  (19 other events, 177.8 us)
where the time goes:
time: 116 us; the launch traced here: 115 us
  Pallas kernels  55.7 us (48%)
  starting transfers between devices  24.9 us (21%)
  waiting for transfers between devices  20.2 us (17%)
  other arithmetic  10.1 us (9%)
  local copies, waits for them, and re-layouts  3.03 us (3%)
    pallas_call x2, Pallas kernels, columns(): kernel_call(functools.partial(columns_kernel, part, parts), 4 + held // M...  15.6 us
    pallas_call x1, Pallas kernels, update(): kernel_call(functools.partial(update_kernel, begins, step, cols, cap, blo...  14 us
    pallas_call x2, Pallas kernels, select(): kernel_call(functools.partial(select_kernel, axis, share, cap, width), 12...  10.4 us
    ppermute x3, waiting for transfers between devices, per_device(): down = lax.ppermute(down, 'col', back)  10.2 us
    pallas_call x3, Pallas kernels, place(): kernel_call(functools.partial(place_kernel, steps, cols, cap), 6, 0, 12 *...  9.07 us
    ppermute x1, waiting for transfers between devices, per_device(): down = lax.ppermute(shard, 'col', back)  7.49 us
    sort x1, other arithmetic, per_device(): keys = lax.sort(keys, dimension=1)  7.33 us
    ppermute x9, starting transfers between devices, swapped(): lax.ppermute(x, axis, [(i, i ^ distance) for i in range(lax.axis_size(axi...  6.5 us
  transfers between devices with their start and end apart: 18, of which 6 were waited for; matrix products, arithmetic and copies ran while one was open for 10% of the time, Pallas kernels for 32%

commit v1 on v0

--- a/solution.py
+++ b/solution.py
@@ -30,6 +30,10 @@
         ys = range(1, side) if turn % 2 == 0 else range(side - 1, 0, -1)
         order += [z * side + y for y in ys]
     return order
+
+
+def row_block(rows, most=400):
+    return max(b for b in range(16, most + 1, 16) if rows % b == 0)
 
 
 def swapped(x, axis, distance):
@@ -135,7 +139,7 @@
     )(order, raw)
 
 
-def filter_rows(toep_ref, pieces, line, out, begin=0):
+def filter_rows(toep_ref, pieces, line, out):
     me = lax.axis_index("row")
     times = toep_ref.shape[0]
     taps = jnp.concatenate([toep_ref[:, times:], toep_ref[:, :times]], 0)
@@ -147,10 +151,9 @@
     @pl.loop(0, rows // block)
     def _(i):
         there = pl.ds(pl.multiple_of(i * block, block), block)
-        source = pl.ds(pl.multiple_of(begin + i * block, math.gcd(begin, block)), block)
         for m, piece in enumerate(pieces):
             at = pl.ds(pl.multiple_of(((m ^ me) + 1) * times, times), times)
-            line[:, at] = piece[source, :]
+            line[:, at] = piece[there, :]
         for s in range(len(pieces)):
             got = jnp.dot(
                 line[:, s * times : (s + 2) * times], both, preferred_element_type=F32
@@ -175,20 +178,27 @@
         out_shape=jax.ShapeDtypeStruct((rows, count * times), BF),
         in_specs=[VM] * (1 + count),
         out_specs=VM,
-        scratch_shapes=[pltpu.VMEM((math.gcd(rows, 256), (count + 1) * times), BF)],
+        scratch_shapes=[pltpu.VMEM((row_block(rows), (count + 1) * times), BF)],
     )(toep, *pieces)
 
 
-def put_rows(list_ref, begin, rows, panel):
-    group = math.gcd(rows.shape[0], 32)
+def put_rows(list_ref, begin, rows, panel, cap=None):
+    group = math.gcd(rows.shape[0], 32 if cap is None else math.gcd(cap, 32))
 
     @pl.loop(0, rows.shape[0] // group)
     def _(g):
         at = pl.multiple_of(g * group, group)
-        to = [list_ref[begin + at + q] for q in range(group)]
-        values = rows[pl.ds(at, group), :].astype(F32)
-        for q in range(group):
-            panel[pl.ds(to[q], 1), :] = values[q : q + 1, :]
+
+        def put():
+            to = [list_ref[begin + at + q] for q in range(group)]
+            values = rows[pl.ds(at, group), :].astype(F32)
+            for q in range(group):
+                panel[pl.ds(to[q], 1), :] = values[q : q + 1, :]
+
+        if cap is None:
+            put()
+        else:
+            pl.when(list_ref[begin + at] < panel.shape[0] - 8)(put)
 
 
 def bring(copy):
@@ -209,7 +219,7 @@
         bring(pltpu.make_async_copy(old, panel, sem))
 
     for step, shard in zip(steps, shards):
-        put_rows(list_ref, ring_source(walk_ref, cols, step) * cap, shard, panel)
+        put_rows(list_ref, ring_source(walk_ref, cols, step) * cap, shard, panel, cap)
     put_rows(extra_ref, 0, nuis, panel)
 
 
@@ -229,7 +239,7 @@
 def place_kernel(steps, cols, cap, walk_ref, list_ref, *refs):
     shards, panel = refs[: len(steps)], refs[-1]
     for step, shard in zip(steps, shards):
-        put_rows(list_ref, ring_source(walk_ref, cols, step) * cap, shard, panel)
+        put_rows(list_ref, ring_source(walk_ref, cols, step) * cap, shard, panel, cap)
 
 
 def place(shards, steps, walk, listed, panel, cols, cap):
@@ -266,7 +276,7 @@
     )(up, down)
 
 
-def columns_kernel(part, parts, rounds_ref, list_ref, extra_ref, toep_ref, nuis, old, *refs):
+def columns_kernel(part, parts, cap, rounds_ref, list_ref, extra_ref, toep_ref, nuis, old, *refs):
     first, last = part == 0, part == parts - 1
     if last:
         pieces, (out, panel, acc, line, sem) = refs[:-5], refs[-5:]
@@ -279,8 +289,8 @@
         def _():
             bring(pltpu.make_async_copy(old, panel, sem))
 
-    filter_rows(toep_ref, pieces, line, acc, part * rows)
-    put_rows(list_ref, part * rows, acc, panel)
+    filter_rows(toep_ref, pieces, line, acc)
+    put_rows(list_ref, part * rows, acc, panel, cap)
     if first:
         put_rows(extra_ref, 0, nuis, panel)
     if last:
@@ -290,16 +300,15 @@
             out[:, at : at + size] = panel[at : at + size, :].T.astype(BF)
 
 
-def columns(part, parts, pieces, rounds, listed, extra, nuis, toep, old):
+def columns(part, parts, cap, pieces, rounds, listed, extra, nuis, toep, old):
     rows, times = pieces[0].shape
-    rows //= parts
     count = len(pieces)
     high, span = old.shape
     last = part == parts - 1
     outs = [jax.ShapeDtypeStruct((span, high - 8), BF), jax.ShapeDtypeStruct((high, span), F32)]
     held = 4 * rows * span + sum(2 * p.size for p in pieces[4:])
     return kernel_call(
-        functools.partial(columns_kernel, part, parts),
+        functools.partial(columns_kernel, part, parts, cap),
         4 + held // MIB,
         8 * rows * span * times,
         12 * rows * span,
@@ -309,7 +318,7 @@
         input_output_aliases={} if part == 0 else {5: 1 if last else 0},
         scratch_shapes=[
             pltpu.VMEM((rows, span), F32),
-            pltpu.VMEM((math.gcd(rows, 256), span + times), BF),
+            pltpu.VMEM((row_block(rows), span + times), BF),
             pltpu.SemaphoreType.DMA,
         ],
     )(rounds, listed, extra, toep, nuis, old, *pieces)
@@ -320,7 +329,7 @@
     weights, priors, (_, out, panel, held, sems) = refs[0], refs[1 : 1 + parts], refs[1 + parts :]
     source = ring_source(walk_ref, cols, step) * cap
     for begin, shard in zip(begins, shards):
-        put_rows(list_ref, source + begin, shard, panel)
+        put_rows(list_ref, source + begin, shard, panel, math.gcd(cap, shard.shape[0]))
     slots, wide = held.shape[0], held.shape[2]
     each = priors[0].shape[0] // block
 
@@ -355,8 +364,8 @@
     part, wide = priors[0].shape
     parts, span = len(priors), weights.shape[0]
     high = part * parts
-    block = max(b for b in range(16, 513, 16) if part % b == 0)
-    slots = min(2, high // block)
+    block = max(b for b in range(16, 257, 16) if part % b == 0)
+    slots = min(3, high // block)
     count = len(shards)
     return kernel_call(
         functools.partial(update_kernel, begins, step, cols, cap, block, parts),
@@ -490,9 +499,6 @@
     order2d = ordering.reshape(total // LANES, LANES)
     to_rows = select(raw, order2d, "row", row_share, cap_row, rows, True)
     pieces = [to_rows[0]] + [swapped(to_rows[m], "row", m) for m in range(1, rows)]
-    params = jnp.concatenate([nuisance_vals, arc_index.astype(F32)[None]], 0)
-    params, _ = lax.optimization_barrier((params, to_rows[-1]))
-    params = [params] + [swapped(params, "row", m) for m in range(1, rows)]
     late, _ = lax.optimization_barrier((raw, to_rows[-1]))
     (to_cols,) = select(late, order2d, "col", col_share, cap_col, cols, False)
     toep = toeplitz(filter_taps, times)
@@ -501,6 +507,9 @@
     to_cols, _ = lax.optimization_barrier((to_cols, shard))
     mine = lax.all_to_all(to_cols, "col", 0, 0, tiled=True)
 
+    params = jnp.concatenate([nuisance_vals, arc_index.astype(F32)[None]], 0)
+    params, _ = lax.optimization_barrier((params, shard))
+    params = [params] + [swapped(params, "row", m) for m in range(1, rows)]
     ordering, _ = lax.optimization_barrier((ordering, shard))
     slots = ordering[: width * cols].reshape(cols, width)
     bits = (total - 1).bit_length()
@@ -566,21 +575,24 @@
 
     _, old_rows, old_cols = lax.while_loop(more, again, (jnp.int32(1), *empty))
 
-    parts = {0: mine}
+    split = [{0: piece} for piece in halves_of(mine, mine, mine.shape[0] // 2)]
     distance = rows // 2
     while distance:
-        for m in list(parts):
-            parts[m ^ distance] = swapped(parts[m], "row", distance)
+        for m in list(split[0]):
+            for parts in split:
+                parts[m ^ distance] = swapped(parts[m], "row", distance)
         distance //= 2
 
     steps, half = cols // 2, cap_row // 2
     half -= half % 16
     row_extra = extra_list(low_row, row_share)
     col_extra = extra_list(low_col, col_share)
-    halves = [parts[m] for m in range(rows)]
 
     def column_part(part, panel):
-        return columns(part, 2, halves, rounds, col_list, col_extra, nuis, toep, panel)
+        pieces = [split[part][m] for m in range(rows)]
+        return columns(
+            part, 2, cap_col, pieces, rounds, col_list, col_extra, nuis, toep, panel
+        )
 
     panel = None
     batch, at = [], []
@@ -602,8 +614,9 @@
                     cols,
                     cap_row,
                 )
-            panel = place(batch, at, walk, row_list, panel, cols, cap_row)
-            batch, at = [], []
+            else:
+                panel = place(batch, at, walk, row_list, panel, cols, cap_row)
+                batch, at = [], []
         batch += [up, down]
         at += [(cols - i) % cols, i]
     col_panel = column_part(0, old_cols)

time: 116 us -> 115 us (level)
  waiting for transfers between devices: 20.2 us -> 24.8 us
  Pallas kernels: 55.7 us -> 51.8 us
  other arithmetic: 10.1 us -> 8.15 us
    ppermute x9 -> x12, waiting for transfers between devices: 1.84 us -> 10.8 us  [swapped(): lax.ppermute(x, axis, [(i, i ^ distance) for i in range(lax.axis_size(axi...]
    ppermute x3, waiting for transfers between devices: 10.2 us -> 6.72 us  [per_device(): down = lax.ppermute(down, 'col', back)]
    pallas_call x2, Pallas kernels: 15.6 us -> 12.4 us  [columns(): kernel_call(functools.partial(columns_kernel, part, parts, cap), 4 + held...]
    pallas_call x1, Pallas kernels: 14 us -> 12.5 us  [update(): kernel_call(functools.partial(update_kernel, begins, step, cols, cap, blo...]
    ppermute x9 -> x12, starting transfers between devices: 6.5 us -> 7.68 us  [swapped(): lax.ppermute(x, axis, [(i, i ^ distance) for i in range(lax.axis_size(axi...]
    pallas_call x3 -> x2, Pallas kernels: 9.07 us -> 8.65 us  [place(): kernel_call(functools.partial(place_kernel, steps, cols, cap), 6, 0, 12 *...]
  transfers between devices with their start and end apart: 18 -> 21, of which waited for: 6 -> 4; matrix products, arithmetic and copies ran while one was open for 10% -> 8% of each run, Pallas kernels for 32% -> 30%
where the time goes in v1:
time: 115 us
  Pallas kernels  51.8 us (45%)
  starting transfers between devices  25.6 us (22%)
  waiting for transfers between devices  24.8 us (22%)
  other arithmetic  8.15 us (7%)
  local copies, waits for them, and re-layouts  2.75 us (2%)
    pallas_call x1, Pallas kernels, update(): kernel_call(functools.partial(update_kernel, begins, step, cols, cap, blo...  12.5 us
    pallas_call x2, Pallas kernels, columns(): kernel_call(functools.partial(columns_kernel, part, parts, cap), 4 + held...  12.4 us
    ppermute x12, waiting for transfers between devices, swapped(): lax.ppermute(x, axis, [(i, i ^ distance) for i in range(lax.axis_size(axi...  10.8 us
    pallas_call x2, Pallas kernels, select(): kernel_call(functools.partial(select_kernel, axis, share, cap, width), 12...  10.5 us
    pallas_call x2, Pallas kernels, place(): kernel_call(functools.partial(place_kernel, steps, cols, cap), 6, 0, 12 *...  8.65 us
    ppermute x12, starting transfers between devices, swapped(): lax.ppermute(x, axis, [(i, i ^ distance) for i in range(lax.axis_size(axi...  7.68 us
    sort x1, other arithmetic, per_device(): keys = lax.sort(keys, dimension=1)  7.4 us
    ppermute x1, waiting for transfers between devices, per_device(): down = lax.ppermute(shard, 'col', back)  7.27 us
  transfers between devices with their start and end apart: 21, of which 4 were waited for; matrix products, arithmetic and copies ran while one was open for 8% of the time, Pallas kernels for 30%

profile of v1, /device:TPU:0, one launch (start us, length us, event | category | flops | bytes accessed | tf_op | source)
XLA Modules:
  0.0 114.5 jit_solution(11298829052058171395)
XLA Ops:
  0.0 4.7 %shard_map.73 = (bf16[512,128]{1,0:T(8,128)(2,1)S(1)}, bf16[512,128]{1,0:T(8,128)(2,1)S(1)}, bf16[512,128]{1,0:T(8,128)(2,1)S(1)}, bf16[512,128]{1,0:T(8,128)(2,1)S(1)}) custom-call(s32[112,128]{1,0:T(8,128)} %bitcast.140, bf16[1760,128]{1,0:T(8,128)(2,1)} %bitcast.150), custom_call_target="tpu_custom_call" | custom-call | flops 1879048192 | bytes 974848 | tf_op jit(solution)/shard_map/pallas_call | solution.py:130
  5.3 2.6 %collective-permute-start.1 = (bf16[512,128]{1,0:T(8,128)(2,1)S(1)}, bf16[512,128]{1,0:T(8,128)(2,1)S(1)}, u32[]{:S(2)}, u32[]{:S(2)}) collective-permute-start(bf16[512,128]{1,0:T(8,128)(2,1)S(1)} %get-tuple-element.180), channel_id=1, source_target_pairs={{0,16},{8,24},{16,0},{24,8},{1,17},{9,25},{17,1},{25,9},{2,18},{10... | collective-permute-start | bytes 393224 | tf_op jit(solution)/shard_map/ppermute | solution.py:40
  9.0 5.9 %shard_map.74 = bf16[2304,128]{1,0:T(8,128)(2,1)} custom-call(s32[112,128]{1,0:T(8,128)S(1)} %bitcast.142, bf16[1760,128]{1,0:T(8,128)(2,1)S(1)} %bitcast.152), custom_call_target="tpu_custom_call" | custom-call | flops 2113929216 | bytes 1040384 | tf_op jit(solution)/shard_map/pallas_call | solution.py:130
  15.5 1.7 %collective-permute-start.6 = (bf16[512,512]{1,0:T(8,128)(2,1)S(1)}, bf16[512,512]{1,0:T(8,128)(2,1)S(1)}, u32[]{:S(2)}, u32[]{:S(2)}) collective-permute-start(bf16[512,512]{1,0:T(8,128)(2,1)S(1)} %shard_map.75.refs_4_), channel_id=1, source_target_pairs={{2,0},{4,2},{6,4},{7,6},{5,7},{3,5},{1,3},{0,1},{10,8},{12,10},{14... | collective-permute-start | bytes 1572872 | tf_op jit(solution)/shard_map/ppermute | solution.py:538
  17.6 6.0 %all-to-all-start.4 = ((bf16[8,288,128]{2,1,0:T(8,128)(2,1)}), bf16[8,288,128]{2,1,0:T(8,128)(2,1)S(1)}, u32[]{:S(2)}, u32[]{:S(2)}) async-start(bf16[8,288,128]{2,1,0:T(8,128)(2,1)} %bitcast.20), calls=%async_computation.4 | async-start | bytes 1179648 | tf_op jit(solution)/shard_map/all_to_all | solution.py:508
  23.6 7.3 %collective-permute-done.6.refs_1_ = bf16[512,512]{1,0:T(8,128)(2,1)S(1)} collective-permute-done((bf16[512,512]{1,0:T(8,128)(2,1)S(1)}, bf16[512,512]{1,0:T(8,128)(2,1)S(1)}, u32[]{:S(2)}, u32[]{:S(2)}) %collective-permute-start.6) | collective-permute-done | bytes 524320 | tf_op jit(solution)/shard_map/ppermute | solution.py:538
  30.9 2.8 %collective-permute-start.7 = (bf16[512,512]{1,0:T(8,128)(2,1)S(1)}, bf16[512,512]{1,0:T(8,128)(2,1)}, u32[]{:S(2)}, u32[]{:S(2)}) collective-permute-start(bf16[512,512]{1,0:T(8,128)(2,1)S(1)} %collective-permute-done.6.refs_1_), channel_id=1, source_target_pairs={{2,0},{4,2},{6,4},{7,6},{5,7},{3,5},{1,3},{0,1},{10,8},{12,10},{14... | collective-permute-start | bytes 1572872 | tf_op jit(solution)/shard_map/ppermute | solution.py:602
  33.8 1.6 %collective-permute-start.12 = (f32[5,128]{1,0:T(8,128)S(1)}, f32[5,128]{1,0:T(8,128)S(1)}, u32[]{:S(2)}, u32[]{:S(2)}) collective-permute-start(f32[5,128]{1,0:T(8,128)S(1)} %pad_maximum_fusion.refs_0_), channel_id=1, source_target_pairs={{0,16},{8,24},{16,0},{24,8},{1,17},{9,25},{17,1},{25,9},{2,18},{10... | collective-permute-start | bytes 7688 | tf_op jit(solution)/shard_map/ppermute | solution.py:40
  36.6 7.4 %sort.14 = (s32[16,1760]{1,0:T(8,128)S(1)}, s32[16,1760]{1,0:T(8,128)}) sort(s32[16,1760]{1,0:T(8,128)S(1)} %get-tuple-element.188, s32[16,1760]{1,0:T(8,128)S(1)} %iota.51), dimensions={1}, to_apply=%region_0.0 | sort | flops 422400 | bytes 450560 | tf_op jit(solution)/shard_map/sort | solution.py:539
  44.0 6.7 %collective-permute-done.7.refs_3_ = bf16[512,512]{1,0:T(8,128)(2,1)} collective-permute-done((bf16[512,512]{1,0:T(8,128)(2,1)S(1)}, bf16[512,512]{1,0:T(8,128)(2,1)}, u32[]{:S(2)}, u32[]{:S(2)}) %collective-permute-start.7) | collective-permute-done | bytes 524320 | tf_op jit(solution)/shard_map/ppermute | solution.py:602
  51.3 4.4 %collective-permute-start.5 = (bf16[512,512]{1,0:T(8,128)(2,1)}, bf16[512,512]{1,0:T(8,128)(2,1)S(1)}, u32[]{:S(2)}, u32[]{:S(2)}) collective-permute-start(bf16[512,512]{1,0:T(8,128)(2,1)} %collective-permute-done.4.refs_2_), channel_id=1, source_target_pairs={{0,2},{2,4},{4,6},{6,7},{7,5},{5,3},{3,1},{1,0},{8,10},{10,12},{12... | collective-permute-start | bytes 1572872 | tf_op jit(solution)/shard_map/ppermute | solution.py:601
  56.6 1.4 %collective-permute-start.15 = (bf16[1152,128]{1,0:T(8,128)(2,1)}, bf16[1152,128]{1,0:T(8,128)(2,1)}, u32[]{:S(2)}, u32[]{:S(2)}) collective-permute-start(bf16[1152,128]{1,0:T(8,128)(2,1)} %get-tuple-element.198.refs_0_), channel_id=1, source_target_pairs={{0,16},{8,24},{16,0},{24,8},{1,17},{9,25},{17,1},{25,9},{2,18},{10... | collective-permute-start | bytes 884744 | tf_op jit(solution)/shard_map/ppermute | solution.py:40
  59.5 1.1 %shard_map.78.nuis.refs_0_ = f32[256,512]{1,0:T(8,128)S(1)} custom-call(f32[128,256]{1,0:T(8,128)S(1)} %reshape.343.toep_ref, f32[5,128]{1,0:T(8,128)S(1)} %pad_maximum_fusion.refs_0_, f32[5,128]{1,0:T(8,128)S(1)} %collective-permute-done.11.refs_1_, f32[5,128]{1,0:T(8,128)S(1)} %collective-permute-done.12.refs_2_, f32[5,128]{1,0:T(8,128)S(1)} %collective-permute-done.13.refs_3_), custom_call_target="tpu_custom_call" | custom-call | flops 402653184 | bytes 524288 | tf_op jit(solution)/shard_map/pallas_call | solution.py:413
  60.6 6.1 %collective-permute-done.15.refs_2_ = bf16[1152,128]{1,0:T(8,128)(2,1)} collective-permute-done((bf16[1152,128]{1,0:T(8,128)(2,1)}, bf16[1152,128]{1,0:T(8,128)(2,1)}, u32[]{:S(2)}, u32[]{:S(2)}) %collective-permute-start.15) | collective-permute-done | bytes 294944 | tf_op jit(solution)/shard_map/ppermute | solution.py:40
  66.8 4.6 %collective-permute-done.18.refs_2_ = bf16[1152,128]{1,0:T(8,128)(2,1)} collective-permute-done((bf16[1152,128]{1,0:T(8,128)(2,1)}, bf16[1152,128]{1,0:T(8,128)(2,1)}, u32[]{:S(2)}, u32[]{:S(2)}) %collective-permute-start.18) | collective-permute-done | bytes 294944 | tf_op jit(solution)/shard_map/ppermute | solution.py:40
  71.9 0.9 shard_map.77
  72.8 1.7 %collective-permute-start.9 = (bf16[256,512]{1,0:T(8,128)(2,1)}, bf16[256,512]{1,0:T(8,128)(2,1)}, u32[]{:S(2)}, u32[]{:S(2)}) collective-permute-start(bf16[256,512]{1,0:T(8,128)(2,1)} %get-tuple-element.190), channel_id=1, source_target_pairs={{0,2},{2,4},{4,6},{6,7},{7,5},{5,3},{3,1},{1,0},{8,10},{10,12},{12... | collective-permute-start | bytes 786440 | tf_op jit(solution)/shard_map/ppermute | solution.py:624
  76.1 1.0 copy-done.3
  77.1 3.4 %shard_map.83.refs_4_ = f32[3592,512]{1,0:T(8,128)S(1)} custom-call(s32[1]{0:T(128)} %get-tuple-element.338.rounds_ref, s32[64]{0:T(128)S(1)} %copy-done.10, s32[4096]{0:T(1024)S(1)} %bitcast.129, s32[256]{0:T(256)S(1)} %get-tuple-element.241.extra_ref, f32[256,512]{1,0:T(8,128)S(1)} %shard_map.78.nuis.refs_0_, f32[3592,512]{1,0:T(8,128)} %get-tuple-element.201.refs_1_, ...), custom_call_target="tpu_custom_call" | custom-call | bytes 3145728 | tf_op jit(solution)/shard_map/pallas_call | solution.py:227
  80.6 5.7 %shard_map.84.refs_2_ = f32[3592,512]{1,0:T(8,128)S(1)} custom-call(s32[64]{0:T(128)S(1)} %copy-done.10, s32[4096]{0:T(1024)S(1)} %bitcast.130, bf16[512,512]{1,0:T(8,128)(2,1)S(1)} %copy-done.7, bf16[512,512]{1,0:T(8,128)(2,1)S(1)} %copy-done.5, bf16[512,512]{1,0:T(8,128)(2,1)} %collective-permute-done.4.refs_2_, ...), custom_call_target="tpu_custom_call", output_to_operand_aliasing={{}: (6, {})} | custom-call | bytes 12582912 | tf_op jit(solution)/shard_map/pallas_call | solution.py:246
  86.3 3.0 %shard_map.85.refs_4_ = f32[3592,512]{1,0:T(8,128)S(1)} custom-call(s32[64]{0:T(128)S(1)} %copy-done.10, s32[4096]{0:T(1024)S(1)} %bitcast.131, bf16[512,512]{1,0:T(8,128)(2,1)S(1)} %copy-done.1, bf16[512,512]{1,0:T(8,128)(2,1)S(1)} %collective-permute-done.8.down.refs_1_, f32[3592,512]{1,0:T(8,128)S(1)} %shard_map.84.refs_2_), custom_call_target="tpu_custom_call", output_to_operand_aliasing={{}: (4, {})} | custom-call | bytes 6291456 | tf_op jit(solution)/shard_map/pallas_call | solution.py:246
  89.3 6.3 %shard_map.81.old = f32[1800,512]{1,0:T(8,128)S(1)} custom-call(s32[1]{0:T(128)} %get-tuple-element.338.rounds_ref, s32[2304]{0:T(1024)S(1)} %reshape.347.list_ref.refs_2_, s32[256]{0:T(256)S(1)} %get-tuple-element.242.extra_ref.refs_3_, f32[128,256]{1,0:T(8,128)S(1)} %get-tuple-element.423, f32[256,512]{1,0:T(8,128)S(1)} %shard_map.78.nuis.refs_0_, ...), custom_call_target="tpu_custom_call" | custom-call | flops 603979776 | bytes 7077888 | tf_op jit(solution)/shard_map/pallas_call | solution.py:310
  95.7 6.1 %shard_map.82 = (bf16[512,1792]{1,0:T(8,128)(2,1)S(1)}, f32[1800,512]{1,0:T(8,128)S(1)}) custom-call(s32[1]{0:T(128)} %get-tuple-element.338.rounds_ref, s32[2304]{0:T(1024)S(1)} %reshape.347.list_ref.refs_2_, s32[256]{0:T(256)S(1)} %get-tuple-element.242.extra_ref.refs_3_, f32[128,256]{1,0:T(8,128)S(1)} %get-tuple-element.423, ...), custom_call_target="tpu_custom_call", output_to_operand_aliasing={{1}: (5, {})} | custom-call | flops 603979776 | bytes 7077888 | tf_op jit(solution)/shard_map/pallas_call | solution.py:310
  101.9 12.5 %shard_map.86 = (f32[3584,1792]{1,0:T(8,128)}, f32[3592,512]{1,0:T(8,128)S(1)}) custom-call(s32[64]{0:T(128)S(1)} %copy-done.10, s32[4096]{0:T(1024)S(1)} %bitcast.132, bf16[256,512]{1,0:T(8,128)(2,1)} %collective-permute-done.9.refs_0_, bf16[256,512]{1,0:T(8,128)(2,1)} %collective-permute-done.10.refs_1_, ...), custom_call_target="tpu_custom_call", output_to_operand_aliasing={{1}: (6, {})} | custom-call | flops 6576668672 | bytes 51380224 | tf_op jit(solution)/shard_map/pallas_call | solution.py:370
  (98 shorter events, 9.1 us)
Async XLA Ops:
  4.7 10.1 %collective-permute-start = (bf16[512,128]{1,0:T(8,128)(2,1)S(1)}, bf16[512,128]{1,0:T(8,128)(2,1)S(1)}, u32[]{:S(2)}, u32[]{:S(2)}) collective-permute-start(bf16[512,128]{1,0:T(8,128)(2,1)S(1)} %get-tuple-element.179), channel_id=1, source_target_pairs={{0,8},{8,0},{16,24},{24,16},{1,9},{9,1},{17,25},{25,17},{2,10},{10... | collective-permute-start | bytes 393224 | tf_op jit(solution)/shard_map/ppermute | solution.py:40
  5.3 9.6 %collective-permute-start.1 = (bf16[512,128]{1,0:T(8,128)(2,1)S(1)}, bf16[512,128]{1,0:T(8,128)(2,1)S(1)}, u32[]{:S(2)}, u32[]{:S(2)}) collective-permute-start(bf16[512,128]{1,0:T(8,128)(2,1)S(1)} %get-tuple-element.180), channel_id=1, source_target_pairs={{0,16},{8,24},{16,0},{24,8},{1,17},{9,25},{17,1},{25,9},{2,18},{10... | collective-permute-start | bytes 393224 | tf_op jit(solution)/shard_map/ppermute | solution.py:40
  7.8 7.0 %collective-permute-start.2 = (bf16[512,128]{1,0:T(8,128)(2,1)S(1)}, bf16[512,128]{1,0:T(8,128)(2,1)S(1)}, u32[]{:S(2)}, u32[]{:S(2)}) collective-permute-start(bf16[512,128]{1,0:T(8,128)(2,1)S(1)} %get-tuple-element.181), channel_id=1, source_target_pairs={{0,24},{8,16},{16,8},{24,0},{1,25},{9,17},{17,9},{25,1},{2,26},{10... | collective-permute-start | bytes 393224 | tf_op jit(solution)/shard_map/ppermute | solution.py:40
  15.5 35.8 %copy-start.2 = (bf16[512,512]{1,0:T(8,128)(2,1)}, bf16[512,512]{1,0:T(8,128)(2,1)S(1)}, u32[]{:S(2)}) copy-start(bf16[512,512]{1,0:T(8,128)(2,1)S(1)} %shard_map.75.refs_4_) | copy-start | bytes 1572868
  15.5 15.4 %collective-permute-start.6 = (bf16[512,512]{1,0:T(8,128)(2,1)S(1)}, bf16[512,512]{1,0:T(8,128)(2,1)S(1)}, u32[]{:S(2)}, u32[]{:S(2)}) collective-permute-start(bf16[512,512]{1,0:T(8,128)(2,1)S(1)} %shard_map.75.refs_4_), channel_id=1, source_target_pairs={{2,0},{4,2},{6,4},{7,6},{5,7},{3,5},{1,3},{0,1},{10,8},{12,10},{14... | collective-permute-start | bytes 1572872 | tf_op jit(solution)/shard_map/ppermute | solution.py:538
  17.3 16.4 %collective-permute-start.3 = (bf16[512,512]{1,0:T(8,128)(2,1)S(1)}, bf16[512,512]{1,0:T(8,128)(2,1)S(1)}, u32[]{:S(2)}, u32[]{:S(2)}) collective-permute-start(bf16[512,512]{1,0:T(8,128)(2,1)S(1)} %shard_map.75.refs_4_), channel_id=1, source_target_pairs={{0,2},{2,4},{4,6},{6,7},{7,5},{5,3},{3,1},{1,0},{8,10},{10,12},{12... | collective-permute-start | bytes 1572872 | tf_op jit(solution)/shard_map/ppermute | solution.py:537
  17.6 38.1 %all-to-all-start.4 = ((bf16[8,288,128]{2,1,0:T(8,128)(2,1)}), bf16[8,288,128]{2,1,0:T(8,128)(2,1)S(1)}, u32[]{:S(2)}, u32[]{:S(2)}) async-start(bf16[8,288,128]{2,1,0:T(8,128)(2,1)} %bitcast.20), calls=%async_computation.4 | async-start | bytes 1179648 | tf_op jit(solution)/shard_map/all_to_all | solution.py:508
  30.9 43.9 %copy-start.4 = (bf16[512,512]{1,0:T(8,128)(2,1)}, bf16[512,512]{1,0:T(8,128)(2,1)S(1)}, u32[]{:S(2)}) copy-start(bf16[512,512]{1,0:T(8,128)(2,1)S(1)} %collective-permute-done.6.refs_1_) | copy-start | bytes 1572868
  30.9 19.8 %collective-permute-start.7 = (bf16[512,512]{1,0:T(8,128)(2,1)S(1)}, bf16[512,512]{1,0:T(8,128)(2,1)}, u32[]{:S(2)}, u32[]{:S(2)}) collective-permute-start(bf16[512,512]{1,0:T(8,128)(2,1)S(1)} %collective-permute-done.6.refs_1_), channel_id=1, source_target_pairs={{2,0},{4,2},{6,4},{7,6},{5,7},{3,5},{1,3},{0,1},{10,8},{12,10},{14... | collective-permute-start | bytes 1572872 | tf_op jit(solution)/shard_map/ppermute | solution.py:602
  33.6 41.2 %copy-start.6 = (bf16[512,512]{1,0:T(8,128)(2,1)}, bf16[512,512]{1,0:T(8,128)(2,1)S(1)}, u32[]{:S(2)}) copy-start(bf16[512,512]{1,0:T(8,128)(2,1)S(1)} %collective-permute-done.3.refs_0_) | copy-start | bytes 1572868
  33.6 17.7 %collective-permute-start.4 = (bf16[512,512]{1,0:T(8,128)(2,1)S(1)}, bf16[512,512]{1,0:T(8,128)(2,1)}, u32[]{:S(2)}, u32[]{:S(2)}) collective-permute-start(bf16[512,512]{1,0:T(8,128)(2,1)S(1)} %collective-permute-done.3.refs_0_), channel_id=1, source_target_pairs={{0,2},{2,4},{4,6},{6,7},{7,5},{5,3},{3,1},{1,0},{8,10},{10,12},{12... | collective-permute-start | bytes 1572872 | tf_op jit(solution)/shard_map/ppermute | solution.py:601
  33.7 22.8 %collective-permute-start.13 = (f32[5,128]{1,0:T(8,128)S(1)}, f32[5,128]{1,0:T(8,128)S(1)}, u32[]{:S(2)}, u32[]{:S(2)}) collective-permute-start(f32[5,128]{1,0:T(8,128)S(1)} %pad_maximum_fusion.refs_0_), channel_id=1, source_target_pairs={{0,24},{8,16},{16,8},{24,0},{1,25},{9,17},{17,9},{25,1},{2,26},{10... | collective-permute-start | bytes 7688 | tf_op jit(solution)/shard_map/ppermute | solution.py:40
  33.8 24.1 %collective-permute-start.12 = (f32[5,128]{1,0:T(8,128)S(1)}, f32[5,128]{1,0:T(8,128)S(1)}, u32[]{:S(2)}, u32[]{:S(2)}) collective-permute-start(f32[5,128]{1,0:T(8,128)S(1)} %pad_maximum_fusion.refs_0_), channel_id=1, source_target_pairs={{0,16},{8,24},{16,0},{24,8},{1,17},{9,25},{17,1},{25,9},{2,18},{10... | collective-permute-start | bytes 7688 | tf_op jit(solution)/shard_map/ppermute | solution.py:40
  35.4 22.5 %collective-permute-start.11 = (f32[5,128]{1,0:T(8,128)S(1)}, f32[5,128]{1,0:T(8,128)S(1)}, u32[]{:S(2)}, u32[]{:S(2)}) collective-permute-start(f32[5,128]{1,0:T(8,128)S(1)} %pad_maximum_fusion.refs_0_), channel_id=1, source_target_pairs={{0,8},{8,0},{16,24},{24,16},{1,9},{9,1},{17,25},{25,17},{2,10},{10... | collective-permute-start | bytes 7688 | tf_op jit(solution)/shard_map/ppermute | solution.py:40
  50.7 20.7 %collective-permute-start.8 = (bf16[512,512]{1,0:T(8,128)(2,1)}, bf16[512,512]{1,0:T(8,128)(2,1)S(1)}, u32[]{:S(2)}, u32[]{:S(2)}) collective-permute-start(bf16[512,512]{1,0:T(8,128)(2,1)} %collective-permute-done.7.refs_3_), channel_id=1, source_target_pairs={{2,0},{4,2},{6,4},{7,6},{5,7},{3,5},{1,3},{0,1},{10,8},{12,10},{14... | collective-permute-start | bytes 1572872 | tf_op jit(solution)/shard_map/ppermute | solution.py:602
  51.3 20.6 %collective-permute-start.5 = (bf16[512,512]{1,0:T(8,128)(2,1)}, bf16[512,512]{1,0:T(8,128)(2,1)S(1)}, u32[]{:S(2)}, u32[]{:S(2)}) collective-permute-start(bf16[512,512]{1,0:T(8,128)(2,1)} %collective-permute-done.4.refs_2_), channel_id=1, source_target_pairs={{0,2},{2,4},{4,6},{6,7},{7,5},{5,3},{3,1},{1,0},{8,10},{10,12},{12... | collective-permute-start | bytes 1572872 | tf_op jit(solution)/shard_map/ppermute | solution.py:601
  56.6 10.2 %collective-permute-start.15 = (bf16[1152,128]{1,0:T(8,128)(2,1)}, bf16[1152,128]{1,0:T(8,128)(2,1)}, u32[]{:S(2)}, u32[]{:S(2)}) collective-permute-start(bf16[1152,128]{1,0:T(8,128)(2,1)} %get-tuple-element.198.refs_0_), channel_id=1, source_target_pairs={{0,16},{8,24},{16,0},{24,8},{1,17},{9,25},{17,1},{25,9},{2,18},{10... | collective-permute-start | bytes 884744 | tf_op jit(solution)/shard_map/ppermute | solution.py:40
  57.9 16.6 %collective-permute-start.14 = (bf16[1152,128]{1,0:T(8,128)(2,1)}, bf16[1152,128]{1,0:T(8,128)(2,1)S(1)}, u32[]{:S(2)}, u32[]{:S(2)}) collective-permute-start(bf16[1152,128]{1,0:T(8,128)(2,1)} %get-tuple-element.198.refs_0_), channel_id=1, source_target_pairs={{0,8},{8,0},{16,24},{24,16},{1,9},{9,1},{17,25},{25,17},{2,10},{10... | collective-permute-start | bytes 884744 | tf_op jit(solution)/shard_map/ppermute | solution.py:40
  57.9 13.5 %collective-permute-start.18 = (bf16[1152,128]{1,0:T(8,128)(2,1)}, bf16[1152,128]{1,0:T(8,128)(2,1)}, u32[]{:S(2)}, u32[]{:S(2)}) collective-permute-start(bf16[1152,128]{1,0:T(8,128)(2,1)} %get-tuple-element.199.refs_0_), channel_id=1, source_target_pairs={{0,16},{8,24},{16,0},{24,8},{1,17},{9,25},{17,1},{25,9},{2,18},{10... | collective-permute-start | bytes 884744 | tf_op jit(solution)/shard_map/ppermute | solution.py:40
  66.8 28.9 %collective-permute-start.17 = (bf16[1152,128]{1,0:T(8,128)(2,1)}, bf16[1152,128]{1,0:T(8,128)(2,1)}, u32[]{:S(2)}, u32[]{:S(2)}) collective-permute-start(bf16[1152,128]{1,0:T(8,128)(2,1)} %get-tuple-element.199.refs_0_), channel_id=1, source_target_pairs={{0,8},{8,0},{16,24},{24,16},{1,9},{9,1},{17,25},{25,17},{2,10},{10... | collective-permute-start | bytes 884744 | tf_op jit(solution)/shard_map/ppermute | solution.py:40
  71.4 17.9 %collective-permute-start.16 = (bf16[1152,128]{1,0:T(8,128)(2,1)}, bf16[1152,128]{1,0:T(8,128)(2,1)}, u32[]{:S(2)}, u32[]{:S(2)}) collective-permute-start(bf16[1152,128]{1,0:T(8,128)(2,1)} %collective-permute-done.15.refs_2_), channel_id=1, source_target_pairs={{0,8},{8,0},{16,24},{24,16},{1,9},{9,1},{17,25},{25,17},{2,10},{10... | collective-permute-start | bytes 884744 | tf_op jit(solution)/shard_map/ppermute | solution.py:40
  71.4 24.3 %collective-permute-start.19 = (bf16[1152,128]{1,0:T(8,128)(2,1)}, bf16[1152,128]{1,0:T(8,128)(2,1)}, u32[]{:S(2)}, u32[]{:S(2)}) collective-permute-start(bf16[1152,128]{1,0:T(8,128)(2,1)} %collective-permute-done.18.refs_2_), channel_id=1, source_target_pairs={{0,8},{8,0},{16,24},{24,16},{1,9},{9,1},{17,25},{25,17},{2,10},{10... | collective-permute-start | bytes 884744 | tf_op jit(solution)/shard_map/ppermute | solution.py:40
  72.8 29.0 %collective-permute-start.9 = (bf16[256,512]{1,0:T(8,128)(2,1)}, bf16[256,512]{1,0:T(8,128)(2,1)}, u32[]{:S(2)}, u32[]{:S(2)}) collective-permute-start(bf16[256,512]{1,0:T(8,128)(2,1)} %get-tuple-element.190), channel_id=1, source_target_pairs={{0,2},{2,4},{4,6},{6,7},{7,5},{5,3},{3,1},{1,0},{8,10},{10,12},{12... | collective-permute-start | bytes 786440 | tf_op jit(solution)/shard_map/ppermute | solution.py:624
  74.5 27.3 %collective-permute-start.10 = (bf16[256,512]{1,0:T(8,128)(2,1)}, bf16[256,512]{1,0:T(8,128)(2,1)}, u32[]{:S(2)}, u32[]{:S(2)}) collective-permute-start(bf16[256,512]{1,0:T(8,128)(2,1)} %get-tuple-element.191), channel_id=1, source_target_pairs={{2,0},{4,2},{6,4},{7,6},{5,7},{3,5},{1,3},{0,1},{10,8},{12,10},{14... | collective-permute-start | bytes 786440 | tf_op jit(solution)/shard_map/ppermute | solution.py:625
  (21 other events, 247.8 us)

commit v2 on v1

--- a/solution.py
+++ b/solution.py
@@ -40,10 +40,11 @@
     return lax.ppermute(x, axis, [(i, i ^ distance) for i in range(lax.axis_size(axis))])
 
 
-def toeplitz(taps, rows):
-    period = 2 * rows + 1
-    padded = jnp.concatenate([taps, jnp.zeros((period - taps.shape[0],), F32)])
-    return jnp.tile(padded, rows)[: rows * 2 * rows].reshape(rows, 2 * rows)
+def toeplitz(taps_ref, times):
+    taps = taps_ref[...]
+    rest = jnp.zeros((1, 2 * times - taps.shape[1]), F32)
+    line = jnp.broadcast_to(jnp.concatenate([taps, rest], 1), (times, 2 * times))
+    return pltpu.roll(line, 0, 1, stride=1, stride_axis=0)
 
 
 def kernel_call(body, limit, flops, moved, **kw):
@@ -139,10 +140,11 @@
     )(order, raw)
 
 
-def filter_rows(toep_ref, pieces, line, out):
+def filter_rows(taps_ref, pieces, line, out):
     me = lax.axis_index("row")
-    times = toep_ref.shape[0]
-    taps = jnp.concatenate([toep_ref[:, times:], toep_ref[:, :times]], 0)
+    times = pieces[0].shape[1]
+    band = toeplitz(taps_ref, times)
+    taps = jnp.concatenate([band[:, times:], band[:, :times]], 0)
     high = taps.astype(BF)
     both = jnp.concatenate([high, (taps - high.astype(F32)).astype(BF)], 1)
     rows, block = out.shape[0], line.shape[0]
@@ -162,9 +164,9 @@
             out[there, s * times : (s + 1) * times] = got.astype(out.dtype)
 
 
-def filter_kernel(toep_ref, *refs):
+def filter_kernel(taps_ref, *refs):
     pieces, out, line = refs[:-2], refs[-2], refs[-1]
-    filter_rows(toep_ref, pieces, line, out)
+    filter_rows(taps_ref, pieces, line, out)
 
 
 def filtered(pieces, toep):
@@ -276,7 +278,7 @@
     )(up, down)
 
 
-def columns_kernel(part, parts, cap, rounds_ref, list_ref, extra_ref, toep_ref, nuis, old, *refs):
+def columns_kernel(part, parts, cap, rounds_ref, list_ref, extra_ref, taps_ref, nuis, old, *refs):
     first, last = part == 0, part == parts - 1
     if last:
         pieces, (out, panel, acc, line, sem) = refs[:-5], refs[-5:]
@@ -289,7 +291,7 @@
         def _():
             bring(pltpu.make_async_copy(old, panel, sem))
 
-    filter_rows(toep_ref, pieces, line, acc)
+    filter_rows(taps_ref, pieces, line, acc)
     put_rows(list_ref, part * rows, acc, panel, cap)
     if first:
         put_rows(extra_ref, 0, nuis, panel)
@@ -386,11 +388,12 @@
     )(walk, listed, *shards, weights, *priors, panel)[0]
 
 
-def nuisance_kernel(toep_ref, *refs):
+def nuisance_kernel(taps_ref, *refs):
     pieces, out, acc = refs[:-2], refs[-2], refs[-1]
     me = lax.axis_index("row")
     lines, times = pieces[0].shape
     count, params = out.shape[0], lines - 1
+    band = toeplitz(taps_ref, times)
     column = lax.broadcasted_iota(I32, (count, times), 0)
     owner = (column // params).astype(F32)
     acc[...] = jnp.zeros_like(acc)
@@ -400,7 +403,7 @@
             picked = jnp.where(lax.rem(column, params) == q, piece[q : q + 1, :], picked)
         raw = jnp.where(piece[params:lines, :] == owner, picked, 0.0)
         got = jnp.dot(
-            raw, toep_ref[...], precision=lax.Precision.HIGHEST, preferred_element_type=F32
+            raw, band, precision=lax.Precision.HIGHEST, preferred_element_type=F32
         )
         at = pl.ds(pl.multiple_of((m ^ me) * times, times), 2 * times)
         acc[:, at] = acc[:, at] + got
@@ -501,7 +504,7 @@
     pieces = [to_rows[0]] + [swapped(to_rows[m], "row", m) for m in range(1, rows)]
     late, _ = lax.optimization_barrier((raw, to_rows[-1]))
     (to_cols,) = select(late, order2d, "col", col_share, cap_col, cols, False)
-    toep = toeplitz(filter_taps, times)
+    toep = filter_taps.reshape(1, -1)
     *pieces, _ = lax.optimization_barrier((*pieces, to_cols))
     shard = filtered(pieces, toep)
     to_cols, _ = lax.optimization_barrier((to_cols, shard))
@@ -615,7 +618,10 @@
                     cap_row,
                 )
             else:
-                panel = place(batch, at, walk, row_list, panel, cols, cap_row)
+                for j in range(0, len(batch), 2):
+                    panel = place(
+                        batch[j : j + 2], at[j : j + 2], walk, row_list, panel, cols, cap_row
+                    )
                 batch, at = [], []
         batch += [up, down]
         at += [(cols - i) % cols, i]

time: 115 us -> 115 us (level)
  Pallas kernels: 51.8 us -> 53.5 us
    pallas_call x2 -> x3, Pallas kernels: 8.65 us -> 9.47 us  [place(): kernel_call(functools.partial(place_kernel, steps, cols, cap), 6, 0, 12 *...]
  transfers between devices with their start and end apart: 21 -> 21, of which waited for: 4 -> 4; matrix products, arithmetic and copies ran while one was open for 8% -> 7% of each run, Pallas kernels for 30% -> 31%
where the time goes in v2:
time: 115 us
  Pallas kernels  53.5 us (47%)
  starting transfers between devices  25.5 us (22%)
  waiting for transfers between devices  25.3 us (22%)
  other arithmetic  7.45 us (6%)
  local copies, waits for them, and re-layouts  1.7 us (1%)
    pallas_call x1, Pallas kernels, update(): kernel_call(functools.partial(update_kernel, begins, step, cols, cap, blo...  12.5 us
    pallas_call x2, Pallas kernels, columns(): kernel_call(functools.partial(columns_kernel, part, parts, cap), 4 + held...  12.4 us
    pallas_call x2, Pallas kernels, select(): kernel_call(functools.partial(select_kernel, axis, share, cap, width), 12...  11.4 us
    ppermute x12, waiting for transfers between devices, swapped(): lax.ppermute(x, axis, [(i, i ^ distance) for i in range(lax.axis_size(axi...  11.3 us
    pallas_call x3, Pallas kernels, place(): kernel_call(functools.partial(place_kernel, steps, cols, cap), 6, 0, 12 *...  9.47 us
    ppermute x12, starting transfers between devices, swapped(): lax.ppermute(x, axis, [(i, i ^ distance) for i in range(lax.axis_size(axi...  7.7 us
    ppermute x1, waiting for transfers between devices, per_device(): down = lax.ppermute(shard, 'col', back)  7.49 us
    sort x1, other arithmetic, per_device(): keys = lax.sort(keys, dimension=1)  7.4 us
  transfers between devices with their start and end apart: 21, of which 4 were waited for; matrix products, arithmetic and copies ran while one was open for 7% of the time, Pallas kernels for 31%

profile of v2, /device:TPU:0, one launch (start us, length us, event | category | flops | bytes accessed | tf_op | source)
XLA Modules:
  0.0 115.0 jit_solution(8600345935586505876)
XLA Ops:
  0.0 4.7 %shard_map.73 = (bf16[512,128]{1,0:T(8,128)(2,1)S(1)}, bf16[512,128]{1,0:T(8,128)(2,1)S(1)}, bf16[512,128]{1,0:T(8,128)(2,1)S(1)}, bf16[512,128]{1,0:T(8,128)(2,1)S(1)}) custom-call(s32[112,128]{1,0:T(8,128)} %bitcast.141, bf16[1760,128]{1,0:T(8,128)(2,1)} %bitcast.155), custom_call_target="tpu_custom_call" | custom-call | flops 1879048192 | bytes 974848 | tf_op jit(solution)/shard_map/pallas_call | solution.py:131
  5.3 2.6 %collective-permute-start.1 = (bf16[512,128]{1,0:T(8,128)(2,1)S(1)}, bf16[512,128]{1,0:T(8,128)(2,1)S(1)}, u32[]{:S(2)}, u32[]{:S(2)}) collective-permute-start(bf16[512,128]{1,0:T(8,128)(2,1)S(1)} %get-tuple-element.180), channel_id=1, source_target_pairs={{0,16},{8,24},{16,0},{24,8},{1,17},{9,25},{17,1},{25,9},{2,18},{10... | collective-permute-start | bytes 393224 | tf_op jit(solution)/shard_map/ppermute | solution.py:40
  7.8 6.8 %shard_map.74 = bf16[2304,128]{1,0:T(8,128)(2,1)} custom-call(s32[112,128]{1,0:T(8,128)} %bitcast.142, bf16[1760,128]{1,0:T(8,128)(2,1)} %bitcast.156), custom_call_target="tpu_custom_call" | custom-call | flops 2113929216 | bytes 1040384 | tf_op jit(solution)/shard_map/pallas_call | solution.py:131
  15.4 1.9 %collective-permute-start.6 = (bf16[512,512]{1,0:T(8,128)(2,1)S(1)}, bf16[512,512]{1,0:T(8,128)(2,1)S(1)}, u32[]{:S(2)}, u32[]{:S(2)}) collective-permute-start(bf16[512,512]{1,0:T(8,128)(2,1)S(1)} %shard_map.75.refs_4_), channel_id=1, source_target_pairs={{2,0},{4,2},{6,4},{7,6},{5,7},{3,5},{1,3},{0,1},{10,8},{12,10},{14... | collective-permute-start | bytes 1572872 | tf_op jit(solution)/shard_map/ppermute | solution.py:541
  17.5 6.1 %all-to-all-start.4 = ((bf16[8,288,128]{2,1,0:T(8,128)(2,1)}), bf16[8,288,128]{2,1,0:T(8,128)(2,1)S(1)}, u32[]{:S(2)}, u32[]{:S(2)}) async-start(bf16[8,288,128]{2,1,0:T(8,128)(2,1)} %bitcast.21), calls=%async_computation.4 | async-start | bytes 1179648 | tf_op jit(solution)/shard_map/all_to_all | solution.py:511
  23.6 7.5 %collective-permute-done.6.refs_1_ = bf16[512,512]{1,0:T(8,128)(2,1)S(1)} collective-permute-done((bf16[512,512]{1,0:T(8,128)(2,1)S(1)}, bf16[512,512]{1,0:T(8,128)(2,1)S(1)}, u32[]{:S(2)}, u32[]{:S(2)}) %collective-permute-start.6) | collective-permute-done | bytes 524320 | tf_op jit(solution)/shard_map/ppermute | solution.py:541
  31.1 2.6 %collective-permute-start.7 = (bf16[512,512]{1,0:T(8,128)(2,1)S(1)}, bf16[512,512]{1,0:T(8,128)(2,1)}, u32[]{:S(2)}, u32[]{:S(2)}) collective-permute-start(bf16[512,512]{1,0:T(8,128)(2,1)S(1)} %collective-permute-done.6.refs_1_), channel_id=1, source_target_pairs={{2,0},{4,2},{6,4},{7,6},{5,7},{3,5},{1,3},{0,1},{10,8},{12,10},{14... | collective-permute-start | bytes 1572872 | tf_op jit(solution)/shard_map/ppermute | solution.py:605
  33.9 1.5 %collective-permute-start.12 = (f32[5,128]{1,0:T(8,128)S(1)}, f32[5,128]{1,0:T(8,128)S(1)}, u32[]{:S(2)}, u32[]{:S(2)}) collective-permute-start(f32[5,128]{1,0:T(8,128)S(1)} %pad_maximum_fusion.refs_0_), channel_id=1, source_target_pairs={{0,16},{8,24},{16,0},{24,8},{1,17},{9,25},{17,1},{25,9},{2,18},{10... | collective-permute-start | bytes 7688 | tf_op jit(solution)/shard_map/ppermute | solution.py:40
  36.6 7.4 %sort.14 = (s32[16,1760]{1,0:T(8,128)S(1)}, s32[16,1760]{1,0:T(8,128)}) sort(s32[16,1760]{1,0:T(8,128)S(1)} %get-tuple-element.188, s32[16,1760]{1,0:T(8,128)S(1)} %iota.51), dimensions={1}, to_apply=%region_0.0 | sort | flops 422400 | bytes 450560 | tf_op jit(solution)/shard_map/sort | solution.py:542
  44.0 6.5 %collective-permute-done.7.refs_1_ = bf16[512,512]{1,0:T(8,128)(2,1)} collective-permute-done((bf16[512,512]{1,0:T(8,128)(2,1)S(1)}, bf16[512,512]{1,0:T(8,128)(2,1)}, u32[]{:S(2)}, u32[]{:S(2)}) %collective-permute-start.7) | collective-permute-done | bytes 524320 | tf_op jit(solution)/shard_map/ppermute | solution.py:605
  51.3 4.2 %collective-permute-start.5 = (bf16[512,512]{1,0:T(8,128)(2,1)}, bf16[512,512]{1,0:T(8,128)(2,1)S(1)}, u32[]{:S(2)}, u32[]{:S(2)}) collective-permute-start(bf16[512,512]{1,0:T(8,128)(2,1)} %collective-permute-done.4.refs_0_), channel_id=1, source_target_pairs={{0,2},{2,4},{4,6},{6,7},{7,5},{5,3},{3,1},{1,0},{8,10},{10,12},{12... | collective-permute-start | bytes 1572872 | tf_op jit(solution)/shard_map/ppermute | solution.py:604
  56.4 1.5 %collective-permute-start.15 = (bf16[1152,128]{1,0:T(8,128)(2,1)}, bf16[1152,128]{1,0:T(8,128)(2,1)}, u32[]{:S(2)}, u32[]{:S(2)}) collective-permute-start(bf16[1152,128]{1,0:T(8,128)(2,1)} %get-tuple-element.198.refs_0_), channel_id=1, source_target_pairs={{0,16},{8,24},{16,0},{24,8},{1,17},{9,25},{17,1},{25,9},{2,18},{10... | collective-permute-start | bytes 884744 | tf_op jit(solution)/shard_map/ppermute | solution.py:40
  58.6 1.2 %shard_map.78.nuis.refs_0_ = f32[256,512]{1,0:T(8,128)S(1)} custom-call(f32[1,128]{1,0:T(1,128)S(1)} %bitcast.153, f32[5,128]{1,0:T(8,128)S(1)} %pad_maximum_fusion.refs_0_, f32[5,128]{1,0:T(8,128)S(1)} %collective-permute-done.11.refs_1_, f32[5,128]{1,0:T(8,128)S(1)} %collective-permute-done.12.refs_2_, f32[5,128]{1,0:T(8,128)S(1)} %collective-permute-done.13.refs_3_), custom_call_target="tpu_custom_call" | custom-call | flops 402653184 | bytes 524288 | tf_op jit(solution)/shard_map/pallas_call | solution.py:416
  59.8 6.8 %collective-permute-done.15.refs_2_ = bf16[1152,128]{1,0:T(8,128)(2,1)} collective-permute-done((bf16[1152,128]{1,0:T(8,128)(2,1)}, bf16[1152,128]{1,0:T(8,128)(2,1)}, u32[]{:S(2)}, u32[]{:S(2)}) %collective-permute-start.15) | collective-permute-done | bytes 294944 | tf_op jit(solution)/shard_map/ppermute | solution.py:40
  66.6 4.5 %collective-permute-done.18.refs_2_ = bf16[1152,128]{1,0:T(8,128)(2,1)} collective-permute-done((bf16[1152,128]{1,0:T(8,128)(2,1)}, bf16[1152,128]{1,0:T(8,128)(2,1)}, u32[]{:S(2)}, u32[]{:S(2)}) %collective-permute-start.18) | collective-permute-done | bytes 294944 | tf_op jit(solution)/shard_map/ppermute | solution.py:40
  72.5 1.7 %collective-permute-start.9 = (bf16[256,512]{1,0:T(8,128)(2,1)}, bf16[256,512]{1,0:T(8,128)(2,1)}, u32[]{:S(2)}, u32[]{:S(2)}) collective-permute-start(bf16[256,512]{1,0:T(8,128)(2,1)} %get-tuple-element.190), channel_id=1, source_target_pairs={{0,2},{2,4},{4,6},{6,7},{7,5},{5,3},{3,1},{1,0},{8,10},{10,12},{12... | collective-permute-start | bytes 786440 | tf_op jit(solution)/shard_map/ppermute | solution.py:630
  75.8 1.0 copy-done.3
  76.8 3.3 %shard_map.83.refs_2_ = f32[3592,512]{1,0:T(8,128)S(1)} custom-call(s32[1]{0:T(128)} %get-tuple-element.338.rounds_ref, s32[64]{0:T(128)S(1)} %copy-done.10, s32[4096]{0:T(1024)S(1)} %bitcast.130, s32[256]{0:T(256)S(1)} %get-tuple-element.241.extra_ref, f32[256,512]{1,0:T(8,128)S(1)} %shard_map.78.nuis.refs_0_, f32[3592,512]{1,0:T(8,128)} %get-tuple-element.424, ...), custom_call_target="tpu_custom_call" | custom-call | bytes 3145728 | tf_op jit(solution)/shard_map/pallas_call | solution.py:229
  80.1 2.9 %shard_map.84.refs_2_ = f32[3592,512]{1,0:T(8,128)S(1)} custom-call(s32[64]{0:T(128)S(1)} %copy-done.10, s32[4096]{0:T(1024)S(1)} %bitcast.131, bf16[512,512]{1,0:T(8,128)(2,1)S(1)} %copy-done.7, bf16[512,512]{1,0:T(8,128)(2,1)S(1)} %copy-done.5, f32[3592,512]{1,0:T(8,128)S(1)} %shard_map.83.refs_2_), custom_call_target="tpu_custom_call", output_to_operand_aliasing={{}: (4, {})} | custom-call | bytes 6291456 | tf_op jit(solution)/shard_map/pallas_call | solution.py:248
  83.1 3.5 %shard_map.85.refs_2_ = f32[3592,512]{1,0:T(8,128)S(1)} custom-call(s32[64]{0:T(128)S(1)} %copy-done.10, s32[4096]{0:T(1024)S(1)} %bitcast.132, bf16[512,512]{1,0:T(8,128)(2,1)} %collective-permute-done.4.refs_0_, bf16[512,512]{1,0:T(8,128)(2,1)} %collective-permute-done.7.refs_1_, f32[3592,512]{1,0:T(8,128)S(1)} %shard_map.84.refs_2_), custom_call_target="tpu_custom_call", output_to_operand_aliasing={{}: (4, {})} | custom-call | bytes 6291456 | tf_op jit(solution)/shard_map/pallas_call | solution.py:248
  86.7 3.0 %shard_map.86.refs_4_ = f32[3592,512]{1,0:T(8,128)S(1)} custom-call(s32[64]{0:T(128)S(1)} %copy-done.10, s32[4096]{0:T(1024)S(1)} %bitcast.133, bf16[512,512]{1,0:T(8,128)(2,1)S(1)} %copy-done.1, bf16[512,512]{1,0:T(8,128)(2,1)S(1)} %collective-permute-done.8.down.refs_1_, f32[3592,512]{1,0:T(8,128)S(1)} %shard_map.85.refs_2_), custom_call_target="tpu_custom_call", output_to_operand_aliasing={{}: (4, {})} | custom-call | bytes 6291456 | tf_op jit(solution)/shard_map/pallas_call | solution.py:248
  89.8 6.3 %shard_map.81.old = f32[1800,512]{1,0:T(8,128)S(1)} custom-call(s32[1]{0:T(128)} %get-tuple-element.338.rounds_ref, s32[2304]{0:T(1024)S(1)} %reshape.346.list_ref.refs_2_, s32[256]{0:T(256)S(1)} %get-tuple-element.242.extra_ref.refs_3_, f32[1,128]{1,0:T(1,128)S(1)} %get-tuple-element.431, f32[256,512]{1,0:T(8,128)S(1)} %shard_map.78.nuis.refs_0_, ...), custom_call_target="tpu_custom_call" | custom-call | flops 603979776 | bytes 7077888 | tf_op jit(solution)/shard_map/pallas_call | solution.py:312
  96.1 6.1 %shard_map.82 = (bf16[512,1792]{1,0:T(8,128)(2,1)S(1)}, f32[1800,512]{1,0:T(8,128)S(1)}) custom-call(s32[1]{0:T(128)} %get-tuple-element.338.rounds_ref, s32[2304]{0:T(1024)S(1)} %reshape.346.list_ref.refs_2_, s32[256]{0:T(256)S(1)} %get-tuple-element.242.extra_ref.refs_3_, f32[1,128]{1,0:T(1,128)S(1)} %get-tuple-element.431, ...), custom_call_target="tpu_custom_call", output_to_operand_aliasing={{1}: (5, {})} | custom-call | flops 603979776 | bytes 7077888 | tf_op jit(solution)/shard_map/pallas_call | solution.py:312
  102.3 12.5 %shard_map.87 = (f32[3584,1792]{1,0:T(8,128)}, f32[3592,512]{1,0:T(8,128)S(1)}) custom-call(s32[64]{0:T(128)S(1)} %copy-done.10, s32[4096]{0:T(1024)S(1)} %bitcast.134, bf16[256,512]{1,0:T(8,128)(2,1)} %collective-permute-done.9.refs_0_, bf16[256,512]{1,0:T(8,128)(2,1)} %collective-permute-done.10.refs_1_, ...), custom_call_target="tpu_custom_call", output_to_operand_aliasing={{1}: (6, {})} | custom-call | flops 6576668672 | bytes 51380224 | tf_op jit(solution)/shard_map/pallas_call | solution.py:372
  (92 shorter events, 8.2 us)
Async XLA Ops:
  4.7 10.0 %collective-permute-start = (bf16[512,128]{1,0:T(8,128)(2,1)S(1)}, bf16[512,128]{1,0:T(8,128)(2,1)S(1)}, u32[]{:S(2)}, u32[]{:S(2)}) collective-permute-start(bf16[512,128]{1,0:T(8,128)(2,1)S(1)} %get-tuple-element.179), channel_id=1, source_target_pairs={{0,8},{8,0},{16,24},{24,16},{1,9},{9,1},{17,25},{25,17},{2,10},{10... | collective-permute-start | bytes 393224 | tf_op jit(solution)/shard_map/ppermute | solution.py:40
  5.3 9.4 %collective-permute-start.1 = (bf16[512,128]{1,0:T(8,128)(2,1)S(1)}, bf16[512,128]{1,0:T(8,128)(2,1)S(1)}, u32[]{:S(2)}, u32[]{:S(2)}) collective-permute-start(bf16[512,128]{1,0:T(8,128)(2,1)S(1)} %get-tuple-element.180), channel_id=1, source_target_pairs={{0,16},{8,24},{16,0},{24,8},{1,17},{9,25},{17,1},{25,9},{2,18},{10... | collective-permute-start | bytes 393224 | tf_op jit(solution)/shard_map/ppermute | solution.py:40
  7.8 6.8 %collective-permute-start.2 = (bf16[512,128]{1,0:T(8,128)(2,1)S(1)}, bf16[512,128]{1,0:T(8,128)(2,1)S(1)}, u32[]{:S(2)}, u32[]{:S(2)}) collective-permute-start(bf16[512,128]{1,0:T(8,128)(2,1)S(1)} %get-tuple-element.181), channel_id=1, source_target_pairs={{0,24},{8,16},{16,8},{24,0},{1,25},{9,17},{17,9},{25,1},{2,26},{10... | collective-permute-start | bytes 393224 | tf_op jit(solution)/shard_map/ppermute | solution.py:40
  15.4 35.9 %copy-start.2 = (bf16[512,512]{1,0:T(8,128)(2,1)}, bf16[512,512]{1,0:T(8,128)(2,1)S(1)}, u32[]{:S(2)}) copy-start(bf16[512,512]{1,0:T(8,128)(2,1)S(1)} %shard_map.75.refs_4_) | copy-start | bytes 1572868
  15.4 15.7 %collective-permute-start.6 = (bf16[512,512]{1,0:T(8,128)(2,1)S(1)}, bf16[512,512]{1,0:T(8,128)(2,1)S(1)}, u32[]{:S(2)}, u32[]{:S(2)}) collective-permute-start(bf16[512,512]{1,0:T(8,128)(2,1)S(1)} %shard_map.75.refs_4_), channel_id=1, source_target_pairs={{2,0},{4,2},{6,4},{7,6},{5,7},{3,5},{1,3},{0,1},{10,8},{12,10},{14... | collective-permute-start | bytes 1572872 | tf_op jit(solution)/shard_map/ppermute | solution.py:541
  17.4 16.4 %collective-permute-start.3 = (bf16[512,512]{1,0:T(8,128)(2,1)S(1)}, bf16[512,512]{1,0:T(8,128)(2,1)S(1)}, u32[]{:S(2)}, u32[]{:S(2)}) collective-permute-start(bf16[512,512]{1,0:T(8,128)(2,1)S(1)} %shard_map.75.refs_4_), channel_id=1, source_target_pairs={{0,2},{2,4},{4,6},{6,7},{7,5},{5,3},{3,1},{1,0},{8,10},{10,12},{12... | collective-permute-start | bytes 1572872 | tf_op jit(solution)/shard_map/ppermute | solution.py:540
  17.5 38.0 %all-to-all-start.4 = ((bf16[8,288,128]{2,1,0:T(8,128)(2,1)}), bf16[8,288,128]{2,1,0:T(8,128)(2,1)S(1)}, u32[]{:S(2)}, u32[]{:S(2)}) async-start(bf16[8,288,128]{2,1,0:T(8,128)(2,1)} %bitcast.21), calls=%async_computation.4 | async-start | bytes 1179648 | tf_op jit(solution)/shard_map/all_to_all | solution.py:511
  31.1 43.4 %copy-start.4 = (bf16[512,512]{1,0:T(8,128)(2,1)}, bf16[512,512]{1,0:T(8,128)(2,1)S(1)}, u32[]{:S(2)}) copy-start(bf16[512,512]{1,0:T(8,128)(2,1)S(1)} %collective-permute-done.6.refs_1_) | copy-start | bytes 1572868
  31.1 19.5 %collective-permute-start.7 = (bf16[512,512]{1,0:T(8,128)(2,1)S(1)}, bf16[512,512]{1,0:T(8,128)(2,1)}, u32[]{:S(2)}, u32[]{:S(2)}) collective-permute-start(bf16[512,512]{1,0:T(8,128)(2,1)S(1)} %collective-permute-done.6.refs_1_), channel_id=1, source_target_pairs={{2,0},{4,2},{6,4},{7,6},{5,7},{3,5},{1,3},{0,1},{10,8},{12,10},{14... | collective-permute-start | bytes 1572872 | tf_op jit(solution)/shard_map/ppermute | solution.py:605
  33.7 40.8 %copy-start.6 = (bf16[512,512]{1,0:T(8,128)(2,1)}, bf16[512,512]{1,0:T(8,128)(2,1)S(1)}, u32[]{:S(2)}) copy-start(bf16[512,512]{1,0:T(8,128)(2,1)S(1)} %collective-permute-done.3.refs_0_) | copy-start | bytes 1572868
  33.7 17.6 %collective-permute-start.4 = (bf16[512,512]{1,0:T(8,128)(2,1)S(1)}, bf16[512,512]{1,0:T(8,128)(2,1)}, u32[]{:S(2)}, u32[]{:S(2)}) collective-permute-start(bf16[512,512]{1,0:T(8,128)(2,1)S(1)} %collective-permute-done.3.refs_0_), channel_id=1, source_target_pairs={{0,2},{2,4},{4,6},{6,7},{7,5},{5,3},{3,1},{1,0},{8,10},{10,12},{12... | collective-permute-start | bytes 1572872 | tf_op jit(solution)/shard_map/ppermute | solution.py:604
  33.8 22.6 %collective-permute-start.13 = (f32[5,128]{1,0:T(8,128)S(1)}, f32[5,128]{1,0:T(8,128)S(1)}, u32[]{:S(2)}, u32[]{:S(2)}) collective-permute-start(f32[5,128]{1,0:T(8,128)S(1)} %pad_maximum_fusion.refs_0_), channel_id=1, source_target_pairs={{0,24},{8,16},{16,8},{24,0},{1,25},{9,17},{17,9},{25,1},{2,26},{10... | collective-permute-start | bytes 7688 | tf_op jit(solution)/shard_map/ppermute | solution.py:40
  33.9 24.0 %collective-permute-start.12 = (f32[5,128]{1,0:T(8,128)S(1)}, f32[5,128]{1,0:T(8,128)S(1)}, u32[]{:S(2)}, u32[]{:S(2)}) collective-permute-start(f32[5,128]{1,0:T(8,128)S(1)} %pad_maximum_fusion.refs_0_), channel_id=1, source_target_pairs={{0,16},{8,24},{16,0},{24,8},{1,17},{9,25},{17,1},{25,9},{2,18},{10... | collective-permute-start | bytes 7688 | tf_op jit(solution)/shard_map/ppermute | solution.py:40
  35.4 22.5 %collective-permute-start.11 = (f32[5,128]{1,0:T(8,128)S(1)}, f32[5,128]{1,0:T(8,128)S(1)}, u32[]{:S(2)}, u32[]{:S(2)}) collective-permute-start(f32[5,128]{1,0:T(8,128)S(1)} %pad_maximum_fusion.refs_0_), channel_id=1, source_target_pairs={{0,8},{8,0},{16,24},{24,16},{1,9},{9,1},{17,25},{25,17},{2,10},{10... | collective-permute-start | bytes 7688 | tf_op jit(solution)/shard_map/ppermute | solution.py:40
  50.6 20.5 %collective-permute-start.8 = (bf16[512,512]{1,0:T(8,128)(2,1)}, bf16[512,512]{1,0:T(8,128)(2,1)S(1)}, u32[]{:S(2)}, u32[]{:S(2)}) collective-permute-start(bf16[512,512]{1,0:T(8,128)(2,1)} %collective-permute-done.7.refs_1_), channel_id=1, source_target_pairs={{2,0},{4,2},{6,4},{7,6},{5,7},{3,5},{1,3},{0,1},{10,8},{12,10},{14... | collective-permute-start | bytes 1572872 | tf_op jit(solution)/shard_map/ppermute | solution.py:605
  51.3 20.3 %collective-permute-start.5 = (bf16[512,512]{1,0:T(8,128)(2,1)}, bf16[512,512]{1,0:T(8,128)(2,1)S(1)}, u32[]{:S(2)}, u32[]{:S(2)}) collective-permute-start(bf16[512,512]{1,0:T(8,128)(2,1)} %collective-permute-done.4.refs_0_), channel_id=1, source_target_pairs={{0,2},{2,4},{4,6},{6,7},{7,5},{5,3},{3,1},{1,0},{8,10},{10,12},{12... | collective-permute-start | bytes 1572872 | tf_op jit(solution)/shard_map/ppermute | solution.py:604
  56.4 10.2 %collective-permute-start.15 = (bf16[1152,128]{1,0:T(8,128)(2,1)}, bf16[1152,128]{1,0:T(8,128)(2,1)}, u32[]{:S(2)}, u32[]{:S(2)}) collective-permute-start(bf16[1152,128]{1,0:T(8,128)(2,1)} %get-tuple-element.198.refs_0_), channel_id=1, source_target_pairs={{0,16},{8,24},{16,0},{24,8},{1,17},{9,25},{17,1},{25,9},{2,18},{10... | collective-permute-start | bytes 884744 | tf_op jit(solution)/shard_map/ppermute | solution.py:40
  57.9 16.3 %collective-permute-start.14 = (bf16[1152,128]{1,0:T(8,128)(2,1)}, bf16[1152,128]{1,0:T(8,128)(2,1)S(1)}, u32[]{:S(2)}, u32[]{:S(2)}) collective-permute-start(bf16[1152,128]{1,0:T(8,128)(2,1)} %get-tuple-element.198.refs_0_), channel_id=1, source_target_pairs={{0,8},{8,0},{16,24},{24,16},{1,9},{9,1},{17,25},{25,17},{2,10},{10... | collective-permute-start | bytes 884744 | tf_op jit(solution)/shard_map/ppermute | solution.py:40
  57.9 13.2 %collective-permute-start.18 = (bf16[1152,128]{1,0:T(8,128)(2,1)}, bf16[1152,128]{1,0:T(8,128)(2,1)}, u32[]{:S(2)}, u32[]{:S(2)}) collective-permute-start(bf16[1152,128]{1,0:T(8,128)(2,1)} %get-tuple-element.199.refs_0_), channel_id=1, source_target_pairs={{0,16},{8,24},{16,0},{24,8},{1,17},{9,25},{17,1},{25,9},{2,18},{10... | collective-permute-start | bytes 884744 | tf_op jit(solution)/shard_map/ppermute | solution.py:40
  66.6 29.5 %collective-permute-start.17 = (bf16[1152,128]{1,0:T(8,128)(2,1)}, bf16[1152,128]{1,0:T(8,128)(2,1)}, u32[]{:S(2)}, u32[]{:S(2)}) collective-permute-start(bf16[1152,128]{1,0:T(8,128)(2,1)} %get-tuple-element.199.refs_0_), channel_id=1, source_target_pairs={{0,8},{8,0},{16,24},{24,16},{1,9},{9,1},{17,25},{25,17},{2,10},{10... | collective-permute-start | bytes 884744 | tf_op jit(solution)/shard_map/ppermute | solution.py:40
  71.1 18.6 %collective-permute-start.16 = (bf16[1152,128]{1,0:T(8,128)(2,1)}, bf16[1152,128]{1,0:T(8,128)(2,1)}, u32[]{:S(2)}, u32[]{:S(2)}) collective-permute-start(bf16[1152,128]{1,0:T(8,128)(2,1)} %collective-permute-done.15.refs_2_), channel_id=1, source_target_pairs={{0,8},{8,0},{16,24},{24,16},{1,9},{9,1},{17,25},{25,17},{2,10},{10... | collective-permute-start | bytes 884744 | tf_op jit(solution)/shard_map/ppermute | solution.py:40
  71.1 25.0 %collective-permute-start.19 = (bf16[1152,128]{1,0:T(8,128)(2,1)}, bf16[1152,128]{1,0:T(8,128)(2,1)}, u32[]{:S(2)}, u32[]{:S(2)}) collective-permute-start(bf16[1152,128]{1,0:T(8,128)(2,1)} %collective-permute-done.18.refs_2_), channel_id=1, source_target_pairs={{0,8},{8,0},{16,24},{24,16},{1,9},{9,1},{17,25},{25,17},{2,10},{10... | collective-permute-start | bytes 884744 | tf_op jit(solution)/shard_map/ppermute | solution.py:40
  72.5 29.8 %collective-permute-start.9 = (bf16[256,512]{1,0:T(8,128)(2,1)}, bf16[256,512]{1,0:T(8,128)(2,1)}, u32[]{:S(2)}, u32[]{:S(2)}) collective-permute-start(bf16[256,512]{1,0:T(8,128)(2,1)} %get-tuple-element.190), channel_id=1, source_target_pairs={{0,2},{2,4},{4,6},{6,7},{7,5},{5,3},{3,1},{1,0},{8,10},{10,12},{12... | collective-permute-start | bytes 786440 | tf_op jit(solution)/shard_map/ppermute | solution.py:630
  74.2 28.1 %collective-permute-start.10 = (bf16[256,512]{1,0:T(8,128)(2,1)}, bf16[256,512]{1,0:T(8,128)(2,1)}, u32[]{:S(2)}, u32[]{:S(2)}) collective-permute-start(bf16[256,512]{1,0:T(8,128)(2,1)} %get-tuple-element.191), channel_id=1, source_target_pairs={{2,0},{4,2},{6,4},{7,6},{5,7},{3,5},{1,3},{0,1},{10,8},{12,10},{14... | collective-permute-start | bytes 786440 | tf_op jit(solution)/shard_map/ppermute | solution.py:631
  (20 other events, 266.6 us)
